TPU v7x, 32 devices: a whole 2x2x4 slice. The times are simulated.
32 devices in a mesh: dp: 4 (over x, core), tensor: 8 (over z, y).
Axes of the slice: x: 2, y: 2, z: 4, core: 2. Of those that a mesh axis runs over, the one named last changes fastest.
Arguments:
- hidden_in: bfloat16 [24576, 768], P(('dp', 'tensor')), may hold values from -6 to 6
- visual_maps: bfloat16 [4704, 256], P(('dp', 'tensor')), may hold values from -63 to 63
- lengths: int32 [32, 3], P(('dp', 'tensor')), may hold values from 50 to 561, as said below
- box_x: int32 [24576], P(('dp', 'tensor')), may hold values from 0 to 1000
- box_y: int32 [24576], P(('dp', 'tensor')), may hold values from 0 to 1000
- cotangent: bfloat16 [24576, 768], P(('dp', 'tensor')), may hold values from -6 to 6
- vis_weight: float32 [256, 768], P('dp', 'tensor'), may hold values from -0.375 to 0.375
- vis_moments: float32 [2, 256, 768], P(None, 'dp', 'tensor'), may hold values from -31.039934 to 39.81312, as said below
- qkv_weight: float32 [768, 2304], P('dp', 'tensor'), may hold values from -0.21650635 to 0.21650635
- qkv_moments: float32 [2, 768, 2304], P(None, 'dp', 'tensor'), may hold values from -6.8977631 to 6.8977631, as said below
- out_weight: float32 [768, 768], P('dp', 'tensor'), may hold values from -0.61237244 to 0.61237244
- out_moments: float32 [2, 768, 768], P(None, 'dp', 'tensor'), may hold values from -13.7955262 to 13.7955262, as said below
- up_weight: float32 [768, 3072], P('dp', 'tensor'), may hold values from -0.21650635 to 0.21650635
- up_moments: float32 [2, 768, 3072], P(None, 'dp', 'tensor'), may hold values from -17.244408 to 17.244408, as said below
- down_weight: float32 [3072, 768], P('tensor', 'dp'), may hold values from -0.108253175 to 0.108253175
- down_moments: float32 [2, 3072, 768], P(None, 'tensor', 'dp'), may hold values from -27.5910525 to 31.45728, as said below
- up_bias: float32 [3072], replicated, may hold values from -3 to 3
- up_bias_moments: float32 [2, 3072], replicated, may hold values from -17.244408 to 17.244408, as said below
- bn_params: float32 [2, 256], replicated, may hold values from 0.5 to 1.5
- bn_moments: float32 [2, 2, 256], replicated, may hold values from -34.488816 to 49.152, as said below
- norm_params: float32 [4, 768], replicated, may hold values from 0.5 to 1.5
- norm_moments: float32 [2, 4, 768], replicated, may hold values from -55.182105 to 125.82912, as said below
- bias_rows: float32 [5, 768], replicated, may hold values from -3 to 3
- bias_moments: float32 [2, 5, 768], replicated, may hold values from -55.182105 to 125.82912, as said below
- rel_tables: float32 [12, 160], replicated, may hold values from -3 to 3
- table_moments: float32 [2, 12, 160], replicated, may hold values from -13.7955262 to 13.7955262, as said below
Outputs:
- block_out: bfloat16 [24576, 768], P(('dp', 'tensor'))
- grad_hidden: float32 [24576, 768], P(('dp', 'tensor'))
- lamb_norms: float32 [3, 10], replicated
- vis_grad: float32 [256, 768], P('dp', 'tensor')
- vis_new: float32 [256, 768], P('dp', 'tensor')
- vis_moments_new: float32 [2, 256, 768], P(None, 'dp', 'tensor')
- vis_copy: bfloat16 [256, 768], P('dp', 'tensor')
- qkv_grad: float32 [768, 2304], P('dp', 'tensor')
- qkv_new: float32 [768, 2304], P('dp', 'tensor')
- qkv_moments_new: float32 [2, 768, 2304], P(None, 'dp', 'tensor')
- qkv_copy: bfloat16 [768, 2304], P('dp', 'tensor')
- out_grad: float32 [768, 768], P('dp', 'tensor')
- out_new: float32 [768, 768], P('dp', 'tensor')
- out_moments_new: float32 [2, 768, 768], P(None, 'dp', 'tensor')
- out_copy: bfloat16 [768, 768], P('dp', 'tensor')
- up_grad: float32 [768, 3072], P('dp', 'tensor')
- up_new: float32 [768, 3072], P('dp', 'tensor')
- up_moments_new: float32 [2, 768, 3072], P(None, 'dp', 'tensor')
- up_copy: bfloat16 [768, 3072], P('dp', 'tensor')
- down_grad: float32 [3072, 768], P('tensor', 'dp')
- down_new: float32 [3072, 768], P('tensor', 'dp')
- down_moments_new: float32 [2, 3072, 768], P(None, 'tensor', 'dp')
- down_copy: bfloat16 [3072, 768], P('tensor', 'dp')
- up_bias_grad: float32 [3072], replicated
- up_bias_new: float32 [3072], replicated
- up_bias_moments_new: float32 [2, 3072], replicated
- up_bias_copy: bfloat16 [3072], replicated
- bn_grad: float32 [2, 256], replicated
- bn_new: float32 [2, 256], replicated
- bn_moments_new: float32 [2, 2, 256], replicated
- bn_copy: bfloat16 [2, 256], replicated
- norm_grad: float32 [4, 768], replicated
- norm_new: float32 [4, 768], replicated
- norm_moments_new: float32 [2, 4, 768], replicated
- norm_copy: bfloat16 [4, 768], replicated
- bias_grad: float32 [5, 768], replicated
- bias_new: float32 [5, 768], replicated
- bias_moments_new: float32 [2, 5, 768], replicated
- bias_copy: bfloat16 [5, 768], replicated
- table_grad: float32 [12, 160], replicated
- table_new: float32 [12, 160], replicated
- table_moments_new: float32 [2, 12, 160], replicated
- table_copy: bfloat16 [12, 160], replicated
Inputs may be any that keep to these rules, and one draw needn't show every extreme that they name: Row b gives the documents of block b in row order; each has at least 50 rows, a row of lengths sums to at most 768, and some document has exactly 561 rows. `vis_moments`: row 1 is positive. `qkv_moments`: row 1 is positive. `out_moments`: row 1 is positive. `up_moments`: row 1 is positive. `down_moments`: row 1 is positive. `up_bias_moments`: row 1 is positive. `bn_moments`: row 1 is positive. `norm_moments`: row 1 is positive. `bias_moments`: row 1 is positive. `table_moments`: row 1 is positive.
All inputs are finite; a program needn't handle non-finite values.
Results may differ from a plain program's by a relative error of at most 0.025.
Values may be sent and summed in bfloat16 or wider, within the bound.
No kernel may reach another device: no remote copies, remote signals or barrier semaphores. Data moves between devices by JAX's collectives and lax.ppermute only.
A program may use at most 448 MiB of HBM per device.

v0:
```python
import math

import jax
import jax.numpy as jnp
from jax import lax
from jax.sharding import PartitionSpec as P

HEADS = 12
HDIM = 64
PATCHES = 49
REL1 = 32
REL2 = 64
DIST1 = 128
DIST2 = 256
STEP = 10


layer_eps = 1e-06
batch_eps = 1e-05
beta_first = 0.9
beta_second = 0.999
adam_eps = 1e-06
weight_decay = 0.01
learn_rate = 0.4
masked_score = -1000000000.0


def contract(left, right, left_dim, right_dim):
    return lax.dot_general(
        left, right, (((left_dim,), (right_dim,)), ((), ())), preferred_element_type=jnp.float32
    )


def exact_gelu(values):
    return jax.nn.gelu(values, approximate=False)


def bucket_edges(bucket_count, max_distance):
    half = bucket_count // 2
    exact = half // 2
    edges = []
    for level in range(1, half):
        if level < exact:
            edges.append(level)
        else:
            found = max_distance
            for distance in range(exact, max_distance + 1):
                if (
                    exact
                    + int(
                        math.log(distance / exact) / math.log(max_distance / exact) * (half - exact)
                    )
                    >= level
                ):
                    found = distance
                    break
            edges.append(found)
    return edges


def bucket_index(delta, bucket_count, max_distance):
    half = bucket_count // 2
    distance = jnp.abs(delta)
    level = jnp.zeros(delta.shape, jnp.int32)
    for edge in bucket_edges(bucket_count, max_distance):
        level = level + (distance >= edge).astype(jnp.int32)
    return (jnp.where(delta > 0, half, 0) + level).astype(jnp.int32)


def pair_ids(box_x, box_y, row_count):
    row_index = jnp.arange(row_count, dtype=jnp.int32)
    linear = bucket_index(row_index[None, :] - row_index[:, None], REL1, DIST1)
    across = bucket_index(box_x[None, :] - box_x[:, None], REL2, DIST2) + REL1
    downward = bucket_index(box_y[None, :] - box_y[:, None], REL2, DIST2) + REL1 + REL2
    return (linear, across, downward)


def block_rows(row_count):
    return 64 if row_count % 64 == 0 else row_count


def one_hot_block(id_triple, start, span_rows):
    columns = jnp.arange(REL1 + 2 * REL2, dtype=jnp.int32)
    total = None
    for ids in id_triple:
        piece = (lax.dynamic_slice_in_dim(ids, start, span_rows, 0)[:, :, None] == columns).astype(
            jnp.bfloat16
        )
        total = piece if total is None else total + piece
    return total.reshape(-1, REL1 + 2 * REL2)


def bias_from_ids(tables, id_triple, row_count):
    high_part = tables.astype(jnp.bfloat16)
    rest_part = tables - high_part.astype(jnp.float32)
    middle_part = rest_part.astype(jnp.bfloat16)
    small_part = (rest_part - middle_part.astype(jnp.float32)).astype(jnp.bfloat16)
    table_parts = jnp.concatenate([high_part, middle_part, small_part], axis=0).T
    span_rows = block_rows(row_count)
    starts = jnp.arange(row_count // span_rows, dtype=jnp.int32) * span_rows

    def bias_one_block(start):
        looked = jnp.dot(
            one_hot_block(id_triple, start, span_rows),
            table_parts,
            preferred_element_type=jnp.float32,
        )
        return jnp.sum(looked.reshape(span_rows, row_count, 3, HEADS), axis=2)

    blocks = lax.map(bias_one_block, starts)
    return jnp.transpose(blocks.reshape(row_count, row_count, HEADS), (2, 0, 1))


def table_grad_from_ids(grad_scores_b, id_triple, row_count):
    span_rows = block_rows(row_count)
    starts = jnp.arange(row_count // span_rows, dtype=jnp.int32) * span_rows

    def table_one_block(start):
        grad_piece = lax.dynamic_slice_in_dim(grad_scores_b, start, span_rows, 1)
        grad_rows = jnp.transpose(grad_piece, (1, 2, 0)).reshape(-1, HEADS)
        return contract(one_hot_block(id_triple, start, span_rows), grad_rows, 0, 0)

    return jnp.sum(lax.map(table_one_block, starts), axis=0).T


def doc_layout(doc_lengths, row_count):
    doc_ends = jnp.cumsum(doc_lengths).astype(jnp.int32)
    doc_count = doc_lengths.shape[0]
    row_index = jnp.arange(row_count, dtype=jnp.int32)
    doc_index = jnp.sum((row_index[:, None] >= doc_ends[None, :]).astype(jnp.int32), axis=1)
    is_valid = doc_index < doc_count
    doc_numbers = jnp.arange(doc_count, dtype=jnp.int32)
    own_end = jnp.sum(
        jnp.where(doc_index[:, None] == doc_numbers[None, :], doc_ends[None, :], 0), axis=1
    )
    offset = row_index - (own_end - PATCHES)
    is_visual = is_valid & (offset >= 0)
    visual_index = jnp.where(is_visual, doc_index * PATCHES + offset, 0).astype(jnp.int32)
    return (doc_index, is_valid, is_visual, visual_index)


def visual_rows(doc_lengths):
    doc_ends = jnp.cumsum(doc_lengths).astype(jnp.int32)
    slot_index = jnp.arange(doc_lengths.shape[0] * PATCHES, dtype=jnp.int32)
    return (jnp.repeat(doc_ends, PATCHES) - PATCHES + slot_index % PATCHES).astype(jnp.int32)


def norm_forward(values, gain_row, shift_row):
    centred = values - jnp.mean(values, axis=-1, keepdims=True)
    inverse = lax.rsqrt(jnp.mean(centred * centred, axis=-1, keepdims=True) + layer_eps)
    normal_hat = centred * inverse
    return (normal_hat * gain_row + shift_row, normal_hat, inverse)


def norm_backward(grad_out, normal_hat, inverse, gain_row):
    scaled = grad_out * gain_row
    grad_in = inverse * (
        scaled
        - jnp.mean(scaled, axis=-1, keepdims=True)
        - normal_hat * jnp.mean(scaled * normal_hat, axis=-1, keepdims=True)
    )
    return (grad_in, jnp.sum(grad_out * normal_hat, axis=0), jnp.sum(grad_out, axis=0))


def lamb_direction(weight, moments, gradient):
    first_moment = beta_first * moments[0] + (1.0 - beta_first) * gradient
    second_moment = beta_second * moments[1] + (1.0 - beta_second) * gradient * gradient
    direction = (
        first_moment
        / (1.0 - beta_first**STEP)
        / (jnp.sqrt(second_moment / (1.0 - beta_second**STEP)) + adam_eps)
        + weight_decay * weight
    )
    return (jnp.stack([first_moment, second_moment]), direction)


def shards(
    hidden_in,
    visual_maps,
    lengths,
    box_x,
    box_y,
    cotangent,
    vis_weight,
    vis_moments,
    qkv_weight,
    qkv_moments,
    out_weight,
    out_moments,
    up_weight,
    up_moments,
    down_weight,
    down_moments,
    up_bias,
    up_bias_moments,
    bn_params,
    bn_moments,
    norm_params,
    norm_moments,
    bias_rows,
    bias_moments,
    rel_tables,
    table_moments,
):
    row_count = hidden_in.shape[0]
    model_width = hidden_in.shape[1]
    device_total = lax.axis_size("dp") * lax.axis_size("tensor")
    doc_lengths = lengths[0]
    doc_index, is_valid, is_visual, visual_index = doc_layout(doc_lengths, row_count)
    vis_cols, qkv_cols, out_cols, up_local, down_local = (
        lax.all_gather(vis_weight.astype(jnp.bfloat16), "dp", axis=0, tiled=True),
        lax.all_gather(qkv_weight.astype(jnp.bfloat16), "dp", axis=0, tiled=True),
        lax.all_gather(out_weight.astype(jnp.bfloat16), "dp", axis=0, tiled=True),
        lax.all_gather(up_weight.astype(jnp.bfloat16), "dp", axis=0, tiled=True),
        lax.all_gather(down_weight.astype(jnp.bfloat16), "dp", axis=1, tiled=True),
    )
    vis_full, qkv_full, out_full = (
        lax.all_gather(vis_cols, "tensor", axis=1, tiled=True),
        lax.all_gather(qkv_cols, "tensor", axis=1, tiled=True),
        lax.all_gather(out_cols, "tensor", axis=1, tiled=True),
    )
    up_use, down_use = (up_local, down_local)
    visual_value = visual_maps.astype(jnp.float32)
    col_sum, col_squares = lax.psum(
        (jnp.sum(visual_value, axis=0), jnp.sum(visual_value * visual_value, axis=0)),
        ("dp", "tensor"),
    )
    total_rows = visual_maps.shape[0] * device_total
    vis_mean = col_sum / total_rows
    vis_var = col_squares / total_rows - vis_mean * vis_mean
    vis_hat = (visual_value - vis_mean) * lax.rsqrt(vis_var + batch_eps)
    normed_b = (vis_hat * bn_params[0] + bn_params[1]).astype(jnp.bfloat16)
    embedded = jnp.dot(normed_b, vis_full, preferred_element_type=jnp.float32) + bias_rows[0]
    mixed_rows = hidden_in.astype(jnp.float32) + jnp.where(
        is_visual[:, None], embedded[visual_index], 0.0
    )
    mixed_b = mixed_rows.astype(jnp.bfloat16)
    qkv_bias = jnp.concatenate([bias_rows[1], jnp.zeros_like(bias_rows[1]), bias_rows[2]])
    projected = (jnp.dot(mixed_b, qkv_full, preferred_element_type=jnp.float32) + qkv_bias).astype(
        jnp.bfloat16
    )
    queries = projected[:, :model_width].reshape(row_count, HEADS, HDIM)
    keys_all = projected[:, model_width : 2 * model_width].reshape(row_count, HEADS, HDIM)
    values_all = projected[:, 2 * model_width :].reshape(row_count, HEADS, HDIM)
    same_doc = (doc_index[:, None] == doc_index[None, :])[None]
    score_scale = HDIM ** (-0.5)
    id_triple = pair_ids(box_x, box_y, row_count)
    rel_bias = bias_from_ids(rel_tables, id_triple, row_count)

    def raw_scores():
        plain_scores = (
            jnp.einsum("qhd,khd->hqk", queries, keys_all, preferred_element_type=jnp.float32)
            * score_scale
        )
        return jnp.where(same_doc, plain_scores + rel_bias, masked_score)

    scores = raw_scores()
    row_max = jnp.max(scores, axis=-1, keepdims=True)
    exp_scores = jnp.exp(scores - row_max)
    row_total = jnp.sum(exp_scores, axis=-1, keepdims=True)
    attn_probs = exp_scores / row_total
    context_b = (
        jnp.einsum(
            "hqk,khd->qhd",
            attn_probs.astype(jnp.bfloat16),
            values_all,
            preferred_element_type=jnp.float32,
        )
        .reshape(row_count, model_width)
        .astype(jnp.bfloat16)
    )
    attended = jnp.dot(context_b, out_full, preferred_element_type=jnp.float32) + bias_rows[3]
    first_norm, first_hat, first_inverse = norm_forward(
        mixed_rows + attended, norm_params[0], norm_params[1]
    )
    first_b = first_norm.astype(jnp.bfloat16)
    hidden_width = up_use.shape[1]
    tensor_index = lax.axis_index("tensor")
    ffn_in = lax.all_gather(first_b, "tensor", axis=0, tiled=True)
    bias_use = lax.dynamic_slice_in_dim(up_bias, tensor_index * hidden_width, hidden_width)
    pre_act = jnp.dot(ffn_in, up_use, preferred_element_type=jnp.float32) + bias_use
    act_b = exact_gelu(pre_act).astype(jnp.bfloat16)
    ffn_out = lax.psum_scatter(
        jnp.dot(
            lax.slice_in_dim(act_b, 0, row_count * lax.axis_size("tensor"), axis=0),
            down_use,
            preferred_element_type=jnp.float32,
        ).astype(jnp.bfloat16),
        "tensor",
        scatter_dimension=0,
        tiled=True,
    ).astype(jnp.float32)
    block_norm, second_hat, second_inverse = norm_forward(
        first_norm + ffn_out + bias_rows[4], norm_params[2], norm_params[3]
    )
    block_out = block_norm.astype(jnp.bfloat16)
    grad_out = cotangent.astype(jnp.float32) * is_valid[:, None].astype(jnp.float32)
    grad_second, gain_two, shift_two = norm_backward(
        grad_out, second_hat, second_inverse, norm_params[2]
    )
    grad_second_b = grad_second.astype(jnp.bfloat16)
    down_bias_grad = jnp.sum(grad_second, axis=0)
    grad_ffn_b = lax.all_gather(grad_second_b, "tensor", axis=0, tiled=True)
    grad_act = contract(grad_ffn_b, down_use, 1, 1)
    gelu_back = jax.vjp(exact_gelu, pre_act)[1]
    grad_pre_b = gelu_back(grad_act)[0].astype(jnp.bfloat16)
    down_grad = contract(act_b, grad_ffn_b, 0, 0)
    up_grad = contract(ffn_in, grad_pre_b, 0, 0)
    up_bias_part = jnp.sum(grad_pre_b.astype(jnp.float32), axis=0)
    up_bias_grad = lax.dynamic_update_slice_in_dim(
        jnp.zeros_like(up_bias), up_bias_part, tensor_index * hidden_width, 0
    )
    ffn_back = lax.psum_scatter(
        contract(
            lax.slice_in_dim(grad_pre_b, 0, row_count * lax.axis_size("tensor"), axis=0),
            up_use,
            1,
            1,
        ).astype(jnp.bfloat16),
        "tensor",
        scatter_dimension=0,
        tiled=True,
    ).astype(jnp.float32)
    grad_first, gain_one, shift_one = norm_backward(
        grad_second + ffn_back, first_hat, first_inverse, norm_params[0]
    )
    grad_attn_b = grad_first.astype(jnp.bfloat16)
    out_bias_grad = jnp.sum(grad_attn_b.astype(jnp.float32), axis=0)
    out_grad = contract(context_b, grad_attn_b, 0, 0)
    grad_context_b = (
        contract(grad_attn_b, out_full, 1, 1).astype(jnp.bfloat16).reshape(row_count, HEADS, HDIM)
    )
    scores = raw_scores()
    attn_probs = jnp.exp(scores - row_max) / row_total
    grad_probs = jnp.einsum(
        "qhd,khd->hqk", grad_context_b, values_all, preferred_element_type=jnp.float32
    )
    grad_scores_b = (
        attn_probs * (grad_probs - jnp.sum(attn_probs * grad_probs, axis=-1, keepdims=True))
    ).astype(jnp.bfloat16)
    grad_queries = (
        jnp.einsum("hqk,khd->qhd", grad_scores_b, keys_all, preferred_element_type=jnp.float32)
        * score_scale
    )
    grad_keys = (
        jnp.einsum("hqk,qhd->khd", grad_scores_b, queries, preferred_element_type=jnp.float32)
        * score_scale
    )
    grad_values = jnp.einsum(
        "hqk,qhd->khd",
        attn_probs.astype(jnp.bfloat16),
        grad_context_b,
        preferred_element_type=jnp.float32,
    )
    masked_grad_b = jnp.where(same_doc, grad_scores_b, jnp.zeros_like(grad_scores_b))
    table_grad = table_grad_from_ids(masked_grad_b, id_triple, row_count)
    grad_projected_b = jnp.concatenate(
        [
            grad_queries.reshape(row_count, model_width),
            grad_keys.reshape(row_count, model_width),
            grad_values.reshape(row_count, model_width),
        ],
        axis=1,
    ).astype(jnp.bfloat16)
    query_bias_grad = jnp.sum(grad_projected_b[:, :model_width].astype(jnp.float32), axis=0)
    value_bias_grad = jnp.sum(grad_projected_b[:, 2 * model_width :].astype(jnp.float32), axis=0)
    qkv_grad = contract(mixed_b, grad_projected_b, 0, 0)
    grad_mixed = grad_first + contract(grad_projected_b, qkv_full, 1, 1)
    grad_embed_b = grad_mixed[visual_rows(doc_lengths)].astype(jnp.bfloat16)
    vis_bias_grad = jnp.sum(grad_embed_b.astype(jnp.float32), axis=0)
    vis_grad = contract(normed_b, grad_embed_b, 0, 0)
    grad_normed = contract(grad_embed_b, vis_full, 1, 1)
    bn_grad = jnp.stack([jnp.sum(grad_normed * vis_hat, axis=0), jnp.sum(grad_normed, axis=0)])
    vis_cols_grad, qkv_cols_grad, out_cols_grad = (
        lax.psum_scatter(
            vis_grad.astype(jnp.bfloat16), "tensor", scatter_dimension=1, tiled=True
        ).astype(jnp.float32),
        lax.psum_scatter(
            qkv_grad.astype(jnp.bfloat16), "tensor", scatter_dimension=1, tiled=True
        ).astype(jnp.float32),
        lax.psum_scatter(
            out_grad.astype(jnp.bfloat16), "tensor", scatter_dimension=1, tiled=True
        ).astype(jnp.float32),
    )
    up_cols_grad, down_cols_grad = (up_grad, down_grad)
    vis_shard, qkv_shard, out_shard, up_shard, down_shard = (
        lax.psum_scatter(
            vis_cols_grad.astype(jnp.bfloat16), "dp", scatter_dimension=0, tiled=True
        ).astype(jnp.float32),
        lax.psum_scatter(
            qkv_cols_grad.astype(jnp.bfloat16), "dp", scatter_dimension=0, tiled=True
        ).astype(jnp.float32),
        lax.psum_scatter(
            out_cols_grad.astype(jnp.bfloat16), "dp", scatter_dimension=0, tiled=True
        ).astype(jnp.float32),
        lax.psum_scatter(
            up_cols_grad.astype(jnp.bfloat16), "dp", scatter_dimension=0, tiled=True
        ).astype(jnp.float32),
        lax.psum_scatter(
            down_cols_grad.astype(jnp.bfloat16), "dp", scatter_dimension=1, tiled=True
        ).astype(jnp.float32),
    )
    norm_grad = jnp.stack([gain_one, shift_one, gain_two, shift_two])
    bias_grad = jnp.stack(
        [vis_bias_grad, query_bias_grad, value_bias_grad, out_bias_grad, down_bias_grad]
    )
    up_bias_total, bn_total, norm_total, bias_total, table_total = lax.psum(
        (up_bias_grad, bn_grad, norm_grad, bias_grad, table_grad), ("dp", "tensor")
    )
    sharded = [
        (vis_weight, vis_moments, vis_shard),
        (qkv_weight, qkv_moments, qkv_shard),
        (out_weight, out_moments, out_shard),
        (up_weight, up_moments, up_shard),
        (down_weight, down_moments, down_shard),
    ]
    whole = [
        (up_bias, up_bias_moments, up_bias_total),
        (bn_params, bn_moments, bn_total),
        (norm_params, norm_moments, norm_total),
        (bias_rows, bias_moments, bias_total),
        (rel_tables, table_moments, table_total),
    ]
    sharded_updates = [lamb_direction(triple[0], triple[1], triple[2]) for triple in sharded]
    whole_updates = [lamb_direction(triple[0], triple[1], triple[2]) for triple in whole]
    local_sums = jnp.stack(
        [
            jnp.stack([jnp.sum(triple[0] * triple[0]) for triple in sharded]),
            jnp.stack([jnp.sum(update[1] * update[1]) for update in sharded_updates]),
        ]
    )
    global_sums = lax.psum(local_sums, ("dp", "tensor"))
    whole_sums = jnp.stack(
        [
            jnp.stack([jnp.sum(triple[0] * triple[0]) for triple in whole]),
            jnp.stack([jnp.sum(update[1] * update[1]) for update in whole_updates]),
        ]
    )
    all_sums = jnp.concatenate([global_sums, whole_sums], axis=1)
    weight_norms = jnp.sqrt(all_sums[0])
    update_norms = jnp.sqrt(all_sums[1])
    trust_ratio = weight_norms / update_norms
    lamb_norms = jnp.stack([weight_norms, update_norms, trust_ratio])
    outputs = [block_out, grad_mixed, lamb_norms]
    triples = sharded + whole
    updates = sharded_updates + whole_updates
    for number in range(10):
        new_weight = triples[number][0] - learn_rate * trust_ratio[number] * updates[number][1]
        outputs.extend(
            [triples[number][2], new_weight, updates[number][0], new_weight.astype(jnp.bfloat16)]
        )
    return tuple(outputs)


def solution(mesh):
    in_specs = (
        P(("dp", "tensor"), None),
        P(("dp", "tensor"), None),
        P(("dp", "tensor"), None),
        P(("dp", "tensor")),
        P(("dp", "tensor")),
        P(("dp", "tensor"), None),
        P("dp", "tensor"),
        P(None, "dp", "tensor"),
        P("dp", "tensor"),
        P(None, "dp", "tensor"),
        P("dp", "tensor"),
        P(None, "dp", "tensor"),
        P("dp", "tensor"),
        P(None, "dp", "tensor"),
        P("tensor", "dp"),
        P(None, "tensor", "dp"),
        P(),
        P(),
        P(),
        P(),
        P(),
        P(),
        P(),
        P(),
        P(),
        P(),
    )
    out_specs = (
        P(("dp", "tensor"), None),
        P(("dp", "tensor"), None),
        P(),
        P("dp", "tensor"),
        P("dp", "tensor"),
        P(None, "dp", "tensor"),
        P("dp", "tensor"),
        P("dp", "tensor"),
        P("dp", "tensor"),
        P(None, "dp", "tensor"),
        P("dp", "tensor"),
        P("dp", "tensor"),
        P("dp", "tensor"),
        P(None, "dp", "tensor"),
        P("dp", "tensor"),
        P("dp", "tensor"),
        P("dp", "tensor"),
        P(None, "dp", "tensor"),
        P("dp", "tensor"),
        P("tensor", "dp"),
        P("tensor", "dp"),
        P(None, "tensor", "dp"),
        P("tensor", "dp"),
        P(),
        P(),
        P(),
        P(),
        P(),
        P(),
        P(),
        P(),
        P(),
        P(),
        P(),
        P(),
        P(),
        P(),
        P(),
        P(),
        P(),
        P(),
        P(),
        P(),
    )
    return jax.shard_map(shards, mesh=mesh, in_specs=in_specs, out_specs=out_specs, check_vma=False)
```

profile of v0, /device:TPU:0, one launch (start us, length us, event | category | flops | bytes accessed | tf_op | source)
XLA Modules:
  0.0 1618.3 jit_solution(13225013015761712600)
XLA Ops:
  40.0 33.5 %all_gather.31 = bf16[256,768]{0,1:T(8,128)(2,1)S(1)} all-gather(bf16[256,96]{0,1:T(8,128)(2,1)S(1)} %copy.274), channel_id=1, replica_groups=mesh['dp'=4,'tensor'=8] {'tensor'}, dimensions={1}, use_global_device_ids=true | all-gather | bytes 442368 | tf_op jit(solution)/shard_map/all_gather | solution.py:218
  75.0 39.0 %all-reduce.1 = (f32[256]{0:T(256)S(1)}, f32[256]{0:T(256)S(1)}) all-reduce(f32[256]{0:T(256)S(1)} %get-tuple-element.381, f32[256]{0:T(256)S(1)} %get-tuple-element.380), channel_id=1, replica_groups=mesh['dp'=4,'tensor'=8] {'dp','tensor'}, use_global_device_ids=true, to_apply=%region_6.7 | all-reduce | flops 512 | bytes 4096 | tf_op jit(solution)/shard_map/psum | solution.py:224
  119.9 16.7 %add_add_fusion.2 = (s32[768,768]{1,0:T(8,128)}, s32[768,768]{1,0:T(8,128)}) fusion(s32[768]{0:T(1024)S(1)} %copy-done.80, s32[768]{0:T(1024)S(1)} %copy-done.81), kind=kLoop, calls=%fused_computation.163 | loop fusion | flops 115605504 | bytes 4724736 | tf_op jit(solution)/shard_map/add | solution.py:74
  136.7 226.8 %while.20 = (s32[]{:T(128)}, f32[12,64,768,12]{2,3,1,0:T(8,128)}, s32[12]{0:T(128)S(1)}, s32[768,768]{1,0:T(8,128)}, s32[768,768]{1,0:T(8,128)}, /*index=5*/s32[...) while((s32[]{:T(128)}, f32[12,64,768,12]{2,3,1,0:T(8,128)}, ...), condition=%wide.region_9.10_spmd, body=%wide.region_7.9_spmd.sunk | while | flops 661782528 | bytes 9668519 | solution.py:110
  141.3 12.4 fusion.274
  160.2 12.4 fusion.274
  292.5 12.4 fusion.274
  363.5 34.6 %copy.281 = f32[768,768,12]{0,1,2:T(8,128)} copy(f32[768,768,12]{1,2,0:T(8,128)} %bitcast.339) | data formatting | bytes 56623104 | tf_op jit(solution)/shard_map/reshape | solution.py:111
  413.1 24.5 %fusion.225 = (f32[12,768]{1,0:T(8,128)S(1)}, f32[12,768,768]{1,2,0:T(8,128)}) fusion(f32[768,768,12]{0,1,2:T(8,128)} %copy.281, pred[768,768]{0,1:T(8,128)(4,1)S(1)} %broadcast_compare_fusion, bf16[768,12,64]{0,2,1:T(8,128)(2,1)S(1)} %bitcast.344, bf16[768,12,64]{0,2,1:T(8,128)(2,1)S(1)} %bitcast.340), kind=kOutput, calls=%fused_computation.403 | convolution fusion | flops 941359872 | bytes 59609088 | tf_op jit(solution)/shard_map/sub | solution.py:259
  437.7 19.0 %fusion.136 = bf16[12,64,768]{2,1,0:T(8,128)(2,1)} fusion(bf16[768,12,64]{0,2,1:T(8,128)(2,1)} %bitcast.352, f32[12,768]{1,0:T(8,128)S(1)} %get-tuple-element.559, f32[768,768,12]{0,1,2:T(8,128)} %copy.281, pred[768,768]{0,1:T(8,128)(4,1)S(1)} %broadcast_compare_fusion, bf16[768,12,64]{0,2,1:T(8,128)(2,1)S(1)} %bitcast.345, ...), kind=kOutput, calls=%fused_computation.190 | convolution fusion | flops 1855006464 | bytes 33656832 | tf_op jit(solution)/shard_map/hqk,khd->qhd/dot_general | solution.py:263
  480.9 120.0 %all-gather.9.cloned.1.call-done = bf16[6144,768]{0,1:T(8,128)(2,1)} async-done(((bf16[768,768]{0,1:T(8,128)(2,1)}), bf16[6144,768]{0,1:T(8,128)(2,1)}) %all-gather.9.cloned.1.call-update) | async-done | bytes 9437200 | tf_op jit(solution)/shard_map/all_gather | solution.py:279
  600.9 28.0 %multiply_convert_fusion.1 = (bf16[6144,384]{1,0:T(8,128)(2,1)S(1)}, f32[6144,384]{1,0:T(8,128)}, f32[6144,384]{1,0:T(8,128)}) fusion(f32[384]{0:T(512)} %dynamic_slice.31, bf16[6144,768]{0,1:T(8,128)(2,1)} %all-gather.9.cloned.1.call-done, bf16[768,384]{1,0:T(8,128)(2,1)S(1)} %all_gather.37), kind=kOutput, calls=%fused_computation.54 | convolution fusion | flops 3779592192 | bytes 33621504 | tf_op jit(solution)/shard_map/dot_general | solution.py:281
  640.3 158.8 %reduce-scatter.17.cloned.1.call-done = bf16[768,768]{0,1:T(8,128)(2,1)} async-done(((bf16[6144,768]{0,1:T(8,128)(2,1)}), bf16[768,768]{0,1:T(8,128)(2,1)}) %reduce-scatter.17.cloned.1.call-update) | async-done | bytes 1179664 | tf_op jit(solution)/shard_map/reduce_scatter | solution.py:283
  806.6 136.6 %all-gather.11.cloned.1.call-done = bf16[6144,768]{0,1:T(8,128)(2,1)} async-done(((bf16[768,768]{0,1:T(8,128)(2,1)}), bf16[6144,768]{0,1:T(8,128)(2,1)}) %all-gather.11.cloned.1.call-update) | async-done | bytes 9437200 | tf_op jit(solution)/shard_map/all_gather | solution.py:303
  943.2 15.5 convert_reduce_fusion
  995.0 133.9 %reduce-scatter.19.cloned.1.call-done = bf16[768,768]{0,1:T(8,128)(2,1)} async-done(((bf16[6144,768]{0,1:T(8,128)(2,1)}), bf16[768,768]{0,1:T(8,128)(2,1)}) %reduce-scatter.19.cloned.1.call-update) | async-done | bytes 1179664 | tf_op jit(solution)/shard_map/reduce_scatter | solution.py:313
  1136.6 21.7 %multiply_reduce_fusion = (f32[12,768]{1,0:T(8,128)S(1)}, f32[12,768,768]{1,2,0:T(8,128)}) fusion(f32[12,768,768]{1,2,0:T(8,128)} %get-tuple-element.560, f32[12,768]{1,0:T(8,128)S(1)} %copy-done.44, bf16[768,12,64]{0,2,1:T(8,128)(2,1)} %bitcast.378, bf16[768,12,64]{0,2,1:T(8,128)(2,1)S(1)} %bitcast.353), kind=kOutput, calls=%fused_computation.44 | convolution fusion | flops 927194112 | bytes 59056128 | tf_op jit(solution)/shard_map/qhd,khd->hqk/dot_general | solution.py:335
  1158.3 23.8 %broadcast_select_fusion = (bf16[12,768,768]{1,2,0:T(8,128)(2,1)}, bf16[12,768,768]{1,2,0:T(8,128)(2,1)S(1)}) fusion(pred[768,768]{0,1:T(8,128)(4,1)S(1)} %copy-done.8, f32[12,768,768]{1,2,0:T(8,128)} %get-tuple-element.565, f32[12,768]{1,0:T(8,128)S(1)} %get-tuple-element.564, f32[12,768,768]{1,2,0:T(8,128)} %get-tuple-element.560, f32[12,768]{1,0:T(8,128)S(1)} %copy-done.44), kind=kLoop, calls=%fused_computation.47 | loop fusion | flops 35389440 | bytes 85598208 | tf_op jit(solution)/shard_map/jit(_where)/select_n | solution.py:355
  1201.0 19.1 %fusion.139 = bf16[12,64,768]{2,1,0:T(8,128)(2,1)} fusion(bf16[768,12,64]{0,2,1:T(8,128)(2,1)} %bitcast.379, f32[12,768]{1,0:T(8,128)S(1)} %copy-done.44, f32[768,768,12]{0,1,2:T(8,128)} %copy.281, pred[768,768]{0,1:T(8,128)(4,1)S(1)} %copy-done.8, bf16[768,12,64]{0,2,1:T(8,128)(2,1)S(1)} %bitcast.347, bf16[768,12,64]{0,2,1:T(8,128)(2,1)S(1)} %bitcast.343), kind=kOutput, calls=%fused_computation.191 | convolution fusion | flops 1855006464 | bytes 33656832 | tf_op jit(solution)/shard_map/hqk,qhd->khd/dot_general | solution.py:349
  1255.8 23.9 %copy.304 = bf16[12,768,768]{2,0,1:T(8,128)(2,1)} copy(bf16[12,768,768]{1,2,0:T(8,128)(2,1)} %get-tuple-element.473) | data formatting | bytes 28311552 | tf_op jit(solution)/shard_map/while | solution.py:123
  1287.3 177.0 %while.21 = (s32[]{:T(128)}, f32[12,160,12]{1,2,0:T(8,128)S(1)}, s32[12]{0:T(128)S(1)}, s32[768,768]{1,0:T(8,128)}, s32[768,768]{1,0:T(8,128)}, /*index=5*/s32[7...) while((s32[]{:T(128)}, f32[12,160,12]{1,2,0:T(8,128)S(1)}, ...), condition=%wide.region_68.69_spmd, body=%wide.region_67.68_spmd.sunk | while | flops 283115520 | bytes 3358891 | solution.py:123
  1487.7 19.9 %reduce-scatter.35.cloned.1.call-done = bf16[192,96]{1,0:T(8,128)(2,1)} async-done(((bf16[768,96]{1,0:T(8,128)(2,1)}), bf16[192,96]{1,0:T(8,128)(2,1)}) %reduce-scatter.35.cloned.1.call-update) | async-done | bytes 36880
  1511.5 21.2 %reduce-scatter.33.cloned.1.call-done = bf16[192,288]{1,0:T(8,128)(2,1)} async-done(((bf16[768,288]{1,0:T(8,128)(2,1)}), bf16[192,288]{1,0:T(8,128)(2,1)}) %reduce-scatter.33.cloned.1.call-update) | async-done | bytes 110608
  1540.1 41.1 %all-reduce = (f32[3072]{0:T(1024)S(1)}, f32[2,256]{1,0:T(2,128)S(1)}, f32[4,768]{1,0:T(4,128)S(1)}, f32[5,768]{1,0:T(8,128)S(1)}, f32[12,160]{1,0:T(8,128)S(1)}, /*index=5*/f32[2,5]{1,0:T(2,128)S(1)}) all-reduce(f32[3072]{0:T(1024)S(1)} %copy-done.67, ...), channel_id=1, replica_groups=mesh['dp'=4,'tensor'=8] {'dp','tensor'}, use_global_device_ids=true, to_apply=%region_48.49 | all-reduce | flops 12426 | bytes 99408 | tf_op jit(solution)/shard_map/psum | solution.py:407
  (565 shorter events, 580.9 us)
Async XLA Ops:
  7.2 393.4 %all-gather.5.cloned.1.call-start = ((), (), s32[]{:S(2)}) async-start(), calls=%async_computation.10 | async-start | bytes 3981312 | tf_op jit(solution)/shard_map/all_gather | solution.py:219
  19.1 437.6 %all-gather.7.cloned.1.call-start = ((), (), s32[]{:S(2)}) async-start(), calls=%async_computation.11 | async-start | bytes 1327104 | tf_op jit(solution)/shard_map/all_gather | solution.py:220
  26.3 574.6 %all-gather.9.cloned.1.call-start = ((), (), s32[]{:S(2)}) async-start(), calls=%async_computation.12 | async-start | bytes 10616832 | tf_op jit(solution)/shard_map/all_gather | solution.py:279
  27.7 409.9 %copy-start.7 = (pred[768,768]{0,1:T(8,128)(4,1)}, pred[768,768]{0,1:T(8,128)(4,1)S(1)}, u32[]{:S(2)}) copy-start(pred[768,768]{0,1:T(8,128)(4,1)S(1)} %broadcast_compare_fusion) | copy-start | bytes 1769476
  32.7 81.7 %copy-start.102 = (f32[1,256]{1,0:T(1,128)}, f32[1,256]{1,0:T(1,128)S(1)}, u32[]{:S(2)}) copy-start(f32[1,256]{1,0:T(1,128)S(1)} %get-tuple-element.543) | copy-start | bytes 3076
  32.7 85.1 %copy-start.100 = (f32[1,256]{1,0:T(1,128)}, f32[1,256]{1,0:T(1,128)S(1)}, u32[]{:S(2)}) copy-start(f32[1,256]{1,0:T(1,128)S(1)} %get-tuple-element.542) | copy-start | bytes 3076
  119.9 278.1 %copy-start.6 = (f32[768,768]{0,1:T(8,128)}, f32[768,768]{0,1:T(8,128)S(1)}, u32[]{:S(2)}) copy-start(f32[768,768]{0,1:T(8,128)S(1)} %copy.275) | copy-start | bytes 7077892
  462.6 336.4 %reduce-scatter.17.cloned.1.call-start = ((), (), s32[]{:S(2)}) async-start(), calls=%async_computation.13 | async-start | bytes 10616832 | tf_op jit(solution)/shard_map/reduce_scatter | solution.py:283
  473.0 155.9 %copy-start.36 = (bf16[384,768]{0,1:T(8,128)(2,1)}, bf16[384,768]{0,1:T(8,128)(2,1)S(1)}, u32[]{:S(2)}) copy-start(bf16[384,768]{0,1:T(8,128)(2,1)S(1)} %all_gather.38) | copy-start | bytes 1769476
  480.9 148.0 %copy-start.34 = (bf16[768,384]{1,0:T(8,128)(2,1)}, bf16[768,384]{1,0:T(8,128)(2,1)S(1)}, u32[]{:S(2)}) copy-start(bf16[768,384]{1,0:T(8,128)(2,1)S(1)} %all_gather.37) | copy-start | bytes 1769476
  638.6 304.6 %all-gather.11.cloned.1.call-start = ((), (), s32[]{:S(2)}) async-start(), calls=%async_computation.14 | async-start | bytes 10616832 | tf_op jit(solution)/shard_map/all_gather | solution.py:303
  803.4 139.8 %copy-start.109 = (f32[384]{0:T(512)S(1)}, f32[384]{0:T(512)}, u32[]{:S(2)}) copy-start(f32[384]{0:T(512)} %dynamic_slice.31) | copy-start | bytes 4612
  806.6 322.3 %reduce-scatter.19.cloned.1.call-start = ((), (), s32[]{:S(2)}) async-start(), calls=%async_computation.15 | async-start | bytes 10616832 | tf_op jit(solution)/shard_map/reduce_scatter | solution.py:313
  968.5 275.6 %reduce-scatter.29.cloned.1.call-start = ((), (), s32[]{:S(2)}) async-start(), calls=%async_computation.20 | async-start | bytes 737280 | tf_op jit(solution)/shard_map/reduce_scatter | solution.py:399
  984.9 260.2 %reduce-scatter.27.cloned.1.call-start = ((), (), s32[]{:S(2)}) async-start(), calls=%async_computation.19 | async-start | bytes 737280 | tf_op jit(solution)/shard_map/reduce_scatter | solution.py:396
  994.7 469.7 %reduce-scatter.21.cloned.1.call-start = ((), (), s32[]{:S(2)}) async-start(), calls=%async_computation.16 | async-start | bytes 442368 | tf_op jit(solution)/shard_map/reduce_scatter | solution.py:375
  1232.5 235.2 %reduce-scatter.25.cloned.1.call-start = ((), (), s32[]{:S(2)}) async-start(), calls=%async_computation.18 | async-start | bytes 1327104 | tf_op jit(solution)/shard_map/reduce_scatter | solution.py:381
  1240.3 231.2 %reduce-scatter.23.cloned.1.call-start = ((), (), s32[]{:S(2)}) async-start(), calls=%async_computation.17 | async-start | bytes 3981312 | tf_op jit(solution)/shard_map/reduce_scatter | solution.py:378
  1286.4 198.4 %reduce-scatter.31.cloned.1.call-start = ((), (), s32[]{:S(2)}) async-start(), calls=%async_computation.21 | async-start | bytes 81920
  1466.0 41.7 %reduce-scatter.35.cloned.1.call-start = ((), (), s32[]{:S(2)}) async-start(), calls=%async_computation.23 | async-start | bytes 245760
  1469.4 63.2 %reduce-scatter.33.cloned.1.call-start = ((), (), s32[]{:S(2)}) async-start(), calls=%async_computation.22 | async-start | bytes 737280
  1471.4 63.2 %copy-start.17 = (f32[192,288]{0,1:T(8,128)S(1)}, f32[192,288]{0,1:T(8,128)}, u32[]{:S(2)}) copy-start(f32[192,288]{0,1:T(8,128)} %copy.297) | copy-start | bytes 663556
  1534.7 64.9 %copy-start.42 = (f32[192,96]{0,1:T(8,128)S(1)}, f32[192,96]{0,1:T(8,128)}, u32[]{:S(2)}) copy-start(f32[192,96]{0,1:T(8,128)} %get-tuple-element.468) | copy-start | bytes 221188
  1536.7 72.9 %copy-start.26 = (f32[384,192]{0,1:T(8,128)S(1)}, f32[384,192]{0,1:T(8,128)}, u32[]{:S(2)}) copy-start(f32[384,192]{0,1:T(8,128)} %get-tuple-element.464) | copy-start | bytes 884740
  (107 other events, 1756.8 us)
Sparse Core Ops, SparseCore 0:
  19.2 70.1 all-gather.4
  92.1 40.5 all-gather.6
  462.8 138.0 all-gather.8
  638.8 160.2 reduce-scatter.16
  806.7 136.4 all-gather.10
  968.6 160.2 reduce-scatter.18
  1132.0 21.1 reduce-scatter.28
  1156.2 22.0 reduce-scatter.26
  1232.6 61.3 reduce-scatter.20
  1297.3 63.7 reduce-scatter.24
  1364.6 78.3 reduce-scatter.22
  1466.1 18.6 reduce-scatter.30
  1487.8 19.7 reduce-scatter.34
  1510.6 22.0 reduce-scatter.32
where the time goes:
time: 1630 us; the launch traced here: 1620 us
  waiting for transfers between devices  602 us (37%)
  matrix products  479 us (29%)
  local copies, waits for them, and re-layouts  226 us (14%)
  blocking collectives  150 us (9%)
  other arithmetic  91.6 us (6%)
  loops' own time  47 us (3%)
  between operations  22.4 us (1%)
    dot_general x22, matrix products, contract(): lax.dot_general(left, right, (((left_dim,), (right_dim,)), ((), ())), pre...  187 us
    reduce_scatter x1, waiting for transfers between devices, shards(): lax.psum_scatter(jnp.dot(lax.slice_in_dim(act_b, 0, row_count * lax.axis_...  159 us
    dot_general x12, matrix products, bias_one_block(): jnp.dot(one_hot_block(id_triple, start, span_rows), table_parts, preferre...  149 us
    all_gather x1, waiting for transfers between devices, shards(): grad_ffn_b = lax.all_gather(grad_second_b, 'tensor', axis=0, tiled=True)  137 us
    reduce_scatter x1, waiting for transfers between devices, shards(): lax.psum_scatter(contract(lax.slice_in_dim(grad_pre_b, 0, row_count * lax...  134 us
    all_gather x1, waiting for transfers between devices, shards(): ffn_in = lax.all_gather(first_b, 'tensor', axis=0, tiled=True)  120 us
    unnamed x17, waiting for transfers between devices  52.4 us
    dynamic_slice x48, local copies, waits for them, and re-layouts, one_hot_block(): lax.dynamic_slice_in_dim(ids, start, span_rows, 0)[:, :, None] == columns  49.3 us
  transfers between devices with their start and end apart: 14, of which 7 were waited for; matrix products, arithmetic and copies ran while one was open for 42% of the time, Pallas kernels for 0%

commit v1 on v0

v1 whole, which is shorter than its diff:
```python
import functools
import math

import jax
import jax.numpy as jnp
import numpy as np
from jax import lax
from jax.experimental import pallas as pl
from jax.experimental.pallas import tpu as pltpu
from jax.sharding import PartitionSpec as P

HEADS = 12
HDIM = 64
PATCHES = 49
REL1 = 32
REL2 = 64
DIST1 = 128
DIST2 = 256
STEP = 10
LANES = 128

layer_eps = 1e-06
batch_eps = 1e-05
beta_first = 0.9
beta_second = 0.999
adam_eps = 1e-06
weight_decay = 0.01
learn_rate = 0.4
masked_score = -1000000000.0
f32 = jnp.float32
bf16 = jnp.bfloat16
SMEM_SPEC = pl.BlockSpec(memory_space=pltpu.SMEM)


def dot_nn(left, right):
    return lax.dot_general(left, right, (((1,), (0,)), ((), ())), preferred_element_type=f32)


def dot_nt(left, right):
    return lax.dot_general(left, right, (((1,), (1,)), ((), ())), preferred_element_type=f32)


def dot_tn(left, right):
    return lax.dot_general(left, right, (((0,), (0,)), ((), ())), preferred_element_type=f32)


def whole_spec(shape):
    zeros = (0,) * len(shape)
    return pl.BlockSpec(tuple(shape), lambda *_: zeros)


def struct(shape, dtype):
    return jax.ShapeDtypeStruct(tuple(shape), dtype)


def bucket_edges(bucket_count, max_distance):
    half = bucket_count // 2
    exact = half // 2
    edges = []
    for level in range(1, half):
        if level < exact:
            edges.append(level)
        else:
            found = max_distance
            for distance in range(exact, max_distance + 1):
                if (
                    exact
                    + int(
                        math.log(distance / exact) / math.log(max_distance / exact) * (half - exact)
                    )
                    >= level
                ):
                    found = distance
                    break
            edges.append(found)
    return edges


EDGES1 = bucket_edges(REL1, DIST1)
EDGES2 = bucket_edges(REL2, DIST2)


def bucket_index(delta, bucket_count, edges):
    half = bucket_count // 2
    exact = half // 2
    distance = jnp.abs(delta)
    level = jnp.minimum(distance, exact)
    for edge in edges[exact:]:
        level = level + (distance >= edge).astype(jnp.int32)
    return jnp.where(delta > 0, half, 0) + level


def doc_ends(lens_ref):
    ends = []
    total = None
    for k in range(lens_ref.shape[1]):
        total = lens_ref[0, k] if total is None else total + lens_ref[0, k]
        ends.append(total)
    return ends


def doc_of(rows, ends):
    found = jnp.zeros(rows.shape, jnp.int32)
    for end in ends:
        found = found + (rows >= end).astype(jnp.int32)
    return found


def visual_mask(rows, ends):
    hit = None
    for end in ends:
        inside = (rows >= end - PATCHES) & (rows < end)
        hit = inside if hit is None else hit | inside
    return hit


def column_of(row_block):
    return jnp.transpose(jnp.broadcast_to(row_block, (LANES, LANES)))


def bias_kernel(lens_ref, xs_ref, ys_ref, xt_ref, yt_ref, tab_ref, out_ref):
    tile = out_ref.shape[1]
    cols_total = out_ref.shape[2]
    ends = doc_ends(lens_ref)
    start = pl.program_id(0) * tile
    rows = lax.broadcasted_iota(jnp.int32, (tile, LANES), 0) + start
    lanes = lax.broadcasted_iota(jnp.int32, (tile, LANES), 1)
    row_doc = doc_of(rows, ends)
    x_col = column_of(xt_ref[...])
    y_col = column_of(yt_ref[...])
    table = tab_ref[...]
    table_lin = jnp.concatenate(
        [table[:, :REL1], jnp.zeros((HEADS, LANES - REL1), f32)], axis=1
    )
    table_xy = table[:, REL1:]

    def one_chunk(c, carry):
        offset = pl.multiple_of(c * LANES, LANES)
        cols = lanes + offset
        lin = bucket_index(cols - rows, REL1, EDGES1)
        across = bucket_index(xs_ref[:, pl.ds(offset, LANES)] - x_col, REL2, EDGES2)
        down = bucket_index(ys_ref[:, pl.ds(offset, LANES)] - y_col, REL2, EDGES2) + REL2
        same = row_doc == doc_of(cols, ends)
        for h in range(HEADS):
            flat_lin = jnp.broadcast_to(table_lin[h : h + 1, :], (tile, LANES))
            flat_xy = jnp.broadcast_to(table_xy[h : h + 1, :], (tile, LANES))
            total = (
                jnp.take_along_axis(flat_lin, lin, axis=1)
                + jnp.take_along_axis(flat_xy, across, axis=1)
                + jnp.take_along_axis(flat_xy, down, axis=1)
            )
            out_ref[h, :, pl.ds(offset, LANES)] = jnp.where(same, total, masked_score).astype(
                out_ref.dtype
            )
        return carry

    lax.fori_loop(0, cols_total // LANES, one_chunk, 0)


def relative_bias(lengths, box_x, box_y, tables):
    rows = box_x.shape[1]
    tile = LANES
    row_spec = pl.BlockSpec((1, tile), lambda i: (0, i))
    return pl.pallas_call(
        bias_kernel,
        grid=(rows // tile,),
        in_specs=[
            SMEM_SPEC,
            whole_spec((1, rows)),
            whole_spec((1, rows)),
            row_spec,
            row_spec,
            whole_spec(tables.shape),
        ],
        out_specs=pl.BlockSpec((HEADS, tile, rows), lambda i: (0, i, 0)),
        out_shape=struct((HEADS, rows, rows), f32),
        name="relative_bias",
    )(lengths, box_x, box_y, box_x, box_y, tables)


def front_kernel(
    lens_ref,
    hidden_ref,
    maps_ref,
    stats_ref,
    bn_ref,
    qo_ref,
    vis_ref,
    bias_ref,
    mixed_ref,
    mixed_b_ref,
    proj_ref,
    wqkv_ref,
    wout_ref,
    normed_ref,
    hat_ref,
    *,
    total_rows,
    qkv_n,
    part_rows,
):
    tile = hidden_ref.shape[0]
    width = hidden_ref.shape[1]
    parts, dp_parts, _, block_n = qo_ref.shape
    out_n = block_n - qkv_n

    @pl.when(pl.program_id(0) == 0)
    def _():
        def one_part(d, carry):
            place = pl.ds(pl.multiple_of(d * part_rows, 16), part_rows)
            for t in range(parts):
                block = qo_ref[t, d, :part_rows, :]
                wqkv_ref[place, t * qkv_n : (t + 1) * qkv_n] = block[:, :qkv_n]
                wout_ref[place, t * out_n : (t + 1) * out_n] = block[:, qkv_n:]
            return carry

        lax.fori_loop(0, dp_parts, one_part, 0)

    ends = doc_ends(lens_ref)
    start = pl.program_id(0) * tile
    visual_total, channels = maps_ref.shape
    rows = lax.broadcasted_iota(jnp.int32, (tile, visual_total), 0) + start
    slots = lax.broadcasted_iota(jnp.int32, (tile, visual_total), 1)
    target = slots
    for k, end in enumerate(ends):
        target = jnp.where(slots >= k * PATCHES, slots - (k + 1) * PATCHES + end, target)
    select = (rows == target).astype(f32).astype(bf16)
    picked = dot_nn(select, maps_ref[...])
    is_visual = visual_mask(
        lax.broadcasted_iota(jnp.int32, (tile, channels), 0) + start, ends
    )
    mean = stats_ref[0:1, :] / total_rows
    var = stats_ref[1:2, :] / total_rows - mean * mean
    hat = (picked - mean) * lax.rsqrt(var + batch_eps)
    hat = jnp.where(is_visual, hat, 0.0)
    hat_ref[...] = hat
    normed = jnp.where(is_visual, hat * bn_ref[0:1, :] + bn_ref[1:2, :], 0.0).astype(bf16)
    normed_ref[...] = normed
    embedded = dot_nn(normed, vis_ref[...]) + bias_ref[0:1, :]
    row_visual = visual_mask(lax.broadcasted_iota(jnp.int32, (tile, width), 0) + start, ends)
    mixed = hidden_ref[...].astype(f32) + jnp.where(row_visual, embedded, 0.0)
    mixed_ref[...] = mixed
    mixed_b = mixed.astype(bf16)
    mixed_b_ref[...] = mixed_b
    for part in range(3):
        columns = slice(part * width, (part + 1) * width)
        piece = dot_nn(mixed_b, wqkv_ref[:, columns])
        if part == 0:
            piece = piece + bias_ref[1:2, :]
        if part == 2:
            piece = piece + bias_ref[2:3, :]
        proj_ref[:, columns] = piece.astype(bf16)


def front(lengths, hidden, maps, stats, bn_params, qo_all, vis_full, bias_rows, total_rows, qkv_n, part_rows):
    rows, width = hidden.shape
    channels = maps.shape[1]
    tile = rows // 3 if rows % 384 == 0 else rows
    row_block = lambda n: pl.BlockSpec((tile, n), lambda i: (i, 0))
    return pl.pallas_call(
        functools.partial(
            front_kernel, total_rows=total_rows, qkv_n=qkv_n, part_rows=part_rows
        ),
        grid=(rows // tile,),
        in_specs=[
            SMEM_SPEC,
            row_block(width),
            whole_spec(maps.shape),
            whole_spec(stats.shape),
            whole_spec(bn_params.shape),
            whole_spec(qo_all.shape),
            whole_spec(vis_full.shape),
            whole_spec(bias_rows.shape),
        ],
        out_specs=[
            row_block(width),
            row_block(width),
            row_block(3 * width),
            whole_spec((width, 3 * width)),
            whole_spec((width, width)),
            row_block(channels),
            row_block(channels),
        ],
        out_shape=[
            struct((rows, width), f32),
            struct((rows, width), bf16),
            struct((rows, 3 * width), bf16),
            struct((width, 3 * width), bf16),
            struct((width, width), bf16),
            struct((rows, channels), bf16),
            struct((rows, channels), f32),
        ],
        name="front",
    )(lengths, hidden, maps, stats, bn_params, qo_all, vis_full, bias_rows)


def pair_mask(shape, h):
    lane = lax.broadcasted_iota(jnp.int32, shape, len(shape) - 1)
    return (lane >= HDIM) if h else (lane < HDIM)


def attend_kernel(q_ref, k_ref, v_ref, bias_ref, ctx_ref, probs_ref):
    queries = q_ref[...].astype(f32) * (HDIM**-0.5)
    context = None
    for h in range(2):
        mask = pair_mask(queries.shape, h)
        query_h = jnp.where(mask, queries, 0.0).astype(bf16)
        scores = dot_nt(query_h, k_ref[...]) + bias_ref[h]
        exps = jnp.exp(scores - jnp.max(scores, axis=-1, keepdims=True))
        probs = (exps * (1.0 / jnp.sum(exps, axis=-1, keepdims=True))).astype(bf16)
        probs_ref[h] = probs
        piece = dot_nn(probs, v_ref[...])
        context = piece if context is None else jnp.where(mask, piece, context)
    ctx_ref[...] = context.astype(bf16)


def attend(projected, bias, rows, width):
    pairs = width // LANES
    tile = rows // 3
    return pl.pallas_call(
        attend_kernel,
        grid=(pairs, rows // tile),
        in_specs=[
            pl.BlockSpec((tile, LANES), lambda p, i: (i, p)),
            pl.BlockSpec((rows, LANES), lambda p, i: (0, pairs + p)),
            pl.BlockSpec((rows, LANES), lambda p, i: (0, 2 * pairs + p)),
            pl.BlockSpec((2, tile, rows), lambda p, i: (p, i, 0)),
        ],
        out_specs=[
            pl.BlockSpec((tile, LANES), lambda p, i: (i, p)),
            pl.BlockSpec((2, tile, rows), lambda p, i: (p, i, 0)),
        ],
        out_shape=[struct((rows, width), bf16), struct((HEADS, rows, rows), bf16)],
        name="attend",
    )(projected, projected, projected, bias)


def attend_back_kernel(q_ref, k_ref, v_ref, ctx_ref, gctx_ref, probs_ref, dq_ref, dk_ref, dv_ref, gs_ref):
    rows = q_ref.shape[0]
    tile = rows // 3
    scale = HDIM**-0.5
    keys_h = []
    for h in range(2):
        mask = pair_mask(k_ref.shape, h)
        keys_h.append(jnp.where(mask, k_ref[...].astype(f32), 0.0).astype(bf16))
    grad_k = None
    grad_v = None
    for i in range(rows // tile):
        place = slice(i * tile, (i + 1) * tile)
        queries = q_ref[place, :].astype(f32) * scale
        grads = gctx_ref[place, :].astype(f32)
        inner = grads * ctx_ref[place, :].astype(f32)
        grad_q = None
        for h in range(2):
            mask = pair_mask(queries.shape, h)
            query_h = jnp.where(mask, queries, 0.0).astype(bf16)
            grad_h = jnp.where(mask, grads, 0.0).astype(bf16)
            total = jnp.sum(jnp.where(mask, inner, 0.0), axis=-1, keepdims=True)
            grad_probs = dot_nt(grad_h, v_ref[...])
            probs = probs_ref[h, place, :]
            grad_scores = (probs.astype(f32) * (grad_probs - total)).astype(bf16)
            gs_ref[h, place, :] = grad_scores
            piece_q = dot_nn(grad_scores, keys_h[h])
            piece_k = dot_tn(grad_scores, query_h)
            piece_v = dot_tn(probs, grad_h)
            grad_q = piece_q if grad_q is None else grad_q + piece_q
            grad_k = piece_k if grad_k is None else grad_k + piece_k
            grad_v = piece_v if grad_v is None else grad_v + piece_v
        dq_ref[place, :] = (grad_q * scale).astype(bf16)
    dk_ref[...] = grad_k.astype(bf16)
    dv_ref[...] = grad_v.astype(bf16)


def attend_back(projected, context, grad_context, probs, first_pair, pair_count):
    rows, width = context.shape
    pairs = width // LANES
    column = lambda shift: pl.BlockSpec((rows, LANES), lambda p: (0, shift + first_pair + p))
    plain = pl.BlockSpec((rows, LANES), lambda p: (0, p))
    n = pair_count
    return pl.pallas_call(
        attend_back_kernel,
        grid=(n,),
        in_specs=[
            column(0),
            column(pairs),
            column(2 * pairs),
            column(0),
            column(0),
            pl.BlockSpec((2, rows, rows), lambda p: (first_pair + p, 0, 0)),
        ],
        out_specs=[plain, plain, plain, pl.BlockSpec((2, rows, rows), lambda p: (p, 0, 0))],
        out_shape=[
            struct((rows, n * LANES), bf16),
            struct((rows, n * LANES), bf16),
            struct((rows, n * LANES), bf16),
            struct((2 * n, rows, rows), bf16),
        ],
        name="attend_back",
    )(projected, projected, projected, context, grad_context, probs)


def table_thetas():
    limits = list(EDGES2) + [1 - edge for edge in EDGES2]
    limits = limits + [5000] * (REL2 - len(limits))
    return np.asarray(limits + limits, np.int32)[None, :]


def table_mix():
    count = len(EDGES2)
    mix = np.zeros((2 * REL2, 2 * REL2), np.float32)
    for side in range(2):
        base = side * REL2
        every = base + 2 * count
        above = lambda m: base + m - 1
        below = lambda m: base + count + m - 1
        for m in range(1, count + 1):
            mix[above(m), base + REL2 // 2 + m] -= 1.0
            if m < count:
                mix[above(m + 1), base + REL2 // 2 + m] += 1.0
            else:
                mix[every, base + REL2 // 2 + m] += 1.0
            mix[below(m), base + m] += 1.0
            if m < count:
                mix[below(m + 1), base + m] -= 1.0
        mix[above(1), base] += 1.0
        mix[below(1), base] -= 1.0
    return mix


def table_plan_kernel(xs_ref, ys_ref, theta_ref, order_ref, spot_ref):
    rows = xs_ref.shape[1]
    chunks = rows // LANES
    lane = lax.broadcasted_iota(jnp.int32, (LANES, LANES), 1)
    sub = lax.broadcasted_iota(jnp.int32, (LANES, LANES), 0)
    wide = 8 * LANES
    for side, line_ref in enumerate((xs_ref, ys_ref)):
        line = line_ref[...]
        below = jnp.zeros((1, wide), f32)
        for c in range(chunks):
            column = column_of(line[:, c * LANES : (c + 1) * LANES])
            rank = jnp.zeros((LANES, 1), f32)
            for e in range(chunks):
                other = line[:, e * LANES : (e + 1) * LANES]
                earlier = (other < column) | (
                    (other == column) & (lane + e * LANES < sub + c * LANES)
                )
                rank = rank + jnp.sum(earlier.astype(f32), axis=1, keepdims=True)
            level = lax.broadcasted_iota(jnp.int32, (LANES, rows), 1).astype(f32)
            order_ref[c * LANES : (c + 1) * LANES, side * rows : (side + 1) * rows] = (
                (rank <= level).astype(f32).astype(bf16)
            )
            steps = lax.broadcasted_iota(jnp.int32, (LANES, wide), 1)
            wide_column = jnp.concatenate([column] * 8, axis=1)
            below = below + jnp.sum((wide_column < steps).astype(f32), axis=0, keepdims=True)
        below_i = below.astype(jnp.int32)
        for c in range(chunks):
            column = column_of(line[:, c * LANES : (c + 1) * LANES])
            limit = jnp.clip(column + theta_ref[...], 0, wide - 1)
            found = jnp.zeros((LANES, LANES), jnp.int32)
            for e in range(8):
                piece = jnp.broadcast_to(below_i[:, e * LANES : (e + 1) * LANES], (LANES, LANES))
                got = jnp.take_along_axis(piece, limit & (LANES - 1), axis=1)
                found = jnp.where((limit >> 7) == e, got, found)
            place = slice(c * LANES, (c + 1) * LANES)
            if side == 0:
                spot_ref[place, :] = found - 1
            else:
                spot_ref[place, :] = jnp.where(lane < REL2, spot_ref[place, :], found - 1)


def table_plan(box_x, box_y):
    rows = box_x.shape[1]
    thetas = jnp.asarray(table_thetas())
    return pl.pallas_call(
        table_plan_kernel,
        grid=(1,),
        in_specs=[whole_spec((1, rows)), whole_spec((1, rows)), whole_spec((1, LANES))],
        out_specs=[whole_spec((rows, 2 * rows)), whole_spec((rows, LANES))],
        out_shape=[struct((rows, 2 * rows), bf16), struct((rows, LANES), jnp.int32)],
        name="table_plan",
    )(box_x, box_y, thetas)


def table_kernel(order_ref, spot_ref, gs_ref, xy_ref, diag_ref):
    rows = gs_ref.shape[1]
    chunks = rows // LANES
    lane = lax.broadcasted_iota(jnp.int32, (LANES, LANES), 1)
    sub = lax.broadcasted_iota(jnp.int32, (LANES, LANES), 0)
    flip = (lane + sub == LANES - 1).astype(f32).astype(bf16)
    total = jnp.zeros((8, LANES), f32)
    diag_ref[...] = jnp.zeros(diag_ref.shape, f32)
    pad = jnp.zeros((LANES, LANES), f32)
    for c in range(chunks):
        place = slice(c * LANES, (c + 1) * LANES)
        grads = gs_ref[0, place, :]
        prefix = dot_nn(grads, order_ref[...])
        spot = spot_ref[place, :]
        low = spot & (LANES - 1)
        high = spot >> 7
        found = jnp.zeros((LANES, LANES), f32)
        for e in range(chunks):
            got_x = jnp.take_along_axis(prefix[:, e * LANES : (e + 1) * LANES], low, axis=1)
            got_y = jnp.take_along_axis(
                prefix[:, rows + e * LANES : rows + (e + 1) * LANES], low, axis=1
            )
            found = jnp.where(high == e, jnp.where(lane < REL2, got_x, got_y), found)
        total = total + jnp.sum(found.reshape(LANES // 8, 8, LANES), axis=0)
        turned = jnp.concatenate([dot_nn(flip, grads), pad], axis=1)
        turned = pltpu.roll(turned, 0, 1, stride=1, stride_axis=0)
        lined = jnp.sum(turned.reshape(LANES // 8, 8, rows + LANES), axis=0)
        first = rows - LANES - c * LANES
        diag_ref[0, :, first : first + rows + LANES] += lined
    xy_ref[0] = total


def table_sums(order, spot, grad_scores, first, heads):
    rows = grad_scores.shape[1]
    return pl.pallas_call(
        table_kernel,
        grid=(heads,),
        in_specs=[
            whole_spec(order.shape),
            whole_spec(spot.shape),
            pl.BlockSpec((1, rows, rows), lambda h: (first + h, 0, 0)),
        ],
        out_specs=[
            pl.BlockSpec((1, 8, LANES), lambda h: (h, 0, 0)),
            pl.BlockSpec((1, 8, 2 * rows), lambda h: (h, 0, 0)),
        ],
        out_shape=[struct((heads, 8, LANES), f32), struct((heads, 8, 2 * rows), f32)],
        name="table_sums",
    )(order, spot, grad_scores)


def table_gradient(xy, diag):
    rows = diag.shape[2] // 2
    sums_xy = jnp.sum(xy, axis=1)
    sums_diag = jnp.sum(diag, axis=1)
    delta = lax.broadcasted_iota(jnp.int32, (2 * rows, REL1), 0) - (rows - 1)
    hot = (
        bucket_index(delta, REL1, EDGES1)
        == lax.broadcasted_iota(jnp.int32, (2 * rows, REL1), 1)
    ).astype(f32)
    exact = functools.partial(
        jnp.dot, precision=lax.Precision.HIGHEST, preferred_element_type=f32
    )
    return jnp.concatenate(
        [exact(sums_diag, hot), exact(sums_xy, jnp.asarray(table_mix()))], axis=1
    )


def row_mean(values):
    return jnp.mean(values, axis=-1, keepdims=True)


def after_kernel(ctx_ref, mixed_ref, wout_ref, bias_ref, norm_ref, first_ref, hat_ref, inv_ref):
    values = mixed_ref[...] + dot_nn(ctx_ref[...], wout_ref[...]) + bias_ref[3:4, :]
    centred = values - row_mean(values)
    inverse = lax.rsqrt(row_mean(centred * centred) + layer_eps)
    hat = centred * inverse
    hat_ref[...] = hat
    inv_ref[...] = inverse
    first_ref[...] = (hat * norm_ref[0:1, :] + norm_ref[1:2, :]).astype(bf16)


def after_attention(context, mixed, w_out, bias_rows, norm_params):
    rows, width = mixed.shape
    tile = rows // 3
    row_block = lambda n: pl.BlockSpec((tile, n), lambda i: (i, 0))
    return pl.pallas_call(
        after_kernel,
        grid=(rows // tile,),
        in_specs=[
            row_block(width),
            row_block(width),
            whole_spec(w_out.shape),
            whole_spec(bias_rows.shape),
            whole_spec(norm_params.shape),
        ],
        out_specs=[row_block(width), row_block(width), row_block(1)],
        out_shape=[
            struct((rows, width), bf16),
            struct((rows, width), f32),
            struct((rows, 1), f32),
        ],
        name="after_attention",
    )(context, mixed, w_out, bias_rows, norm_params)


def joined(ref, width):
    columns = ref.shape[-1]
    return jnp.concatenate([ref[g, :, 0].reshape(width, columns) for g in range(2)], axis=1)


def ffn_kernel(
    lens_ref,
    first_ref,
    up_ref,
    down_ref,
    ubias_ref,
    hat_ref,
    cot_ref,
    norm_ref,
    bias_ref,
    act_ref,
    slope_ref,
    out_ref,
    g2_ref,
    g2b_ref,
    red_ref,
    acc_ref,
):
    step = pl.program_id(0)
    rows, width = first_ref.shape
    block_n = up_ref.shape[-1]
    pre = dot_nn(first_ref[...], joined(up_ref, width)) + ubias_ref[0]
    cdf = 0.5 + 0.5 * lax.erf(pre * (2.0**-0.5))
    act = (pre * cdf).astype(bf16)
    act_ref[0] = act
    slope_ref[0] = (cdf + pre * (jnp.exp(-0.5 * pre * pre) * ((2.0 * math.pi) ** -0.5))).astype(
        bf16
    )
    piece = dot_nt(act, joined(down_ref, width))

    @pl.when(step == 0)
    def _():
        acc_ref[...] = piece

    @pl.when(step > 0)
    def _():
        acc_ref[...] += piece

    @pl.when(step == pl.num_programs(0) - 1)
    def _():
        ends = doc_ends(lens_ref)
        tile = LANES
        red_ref[...] = jnp.zeros(red_ref.shape, f32)

        def one_tile(i, carry):
            place = pl.ds(pl.multiple_of(i * tile, tile), tile)
            values = (
                hat_ref[place, :] * norm_ref[0:1, :]
                + norm_ref[1:2, :]
                + acc_ref[place, :]
                + bias_ref[4:5, :]
            )
            centred = values - row_mean(values)
            inverse = lax.rsqrt(row_mean(centred * centred) + layer_eps)
            hat = centred * inverse
            out_ref[place, :] = (hat * norm_ref[2:3, :] + norm_ref[3:4, :]).astype(bf16)
            row = lax.broadcasted_iota(jnp.int32, (tile, width), 0) + i * tile
            grad = jnp.where(row < ends[-1], cot_ref[place, :].astype(f32), 0.0)
            scaled = grad * norm_ref[2:3, :]
            g2 = inverse * (scaled - row_mean(scaled) - hat * row_mean(scaled * hat))
            g2_ref[place, :] = g2
            g2b_ref[place, :] = g2.astype(bf16)
            red_ref[0:1, :] += jnp.sum(grad * hat, axis=0, keepdims=True)
            red_ref[1:2, :] += jnp.sum(grad, axis=0, keepdims=True)
            red_ref[2:3, :] += jnp.sum(g2, axis=0, keepdims=True)
            return carry

        lax.fori_loop(0, rows // tile, one_tile, 0)


def ffn(lengths, first_b, ud_all, up_bias, hat1, cotangent, norm_params, bias_rows):
    rows, width = first_b.shape
    parts, dp_parts, _, part_rows, block_n = ud_all.shape
    weight = lambda which: pl.BlockSpec(
        (2, dp_parts, 1, part_rows, block_n), lambda t: (t, 0, which, 0, 0)
    )
    block = pl.BlockSpec((1, rows, 2 * block_n), lambda t: (t, 0, 0))
    return pl.pallas_call(
        ffn_kernel,
        grid=(parts // 2,),
        in_specs=[
            SMEM_SPEC,
            whole_spec(first_b.shape),
            weight(0),
            weight(1),
            pl.BlockSpec((1, 1, 2 * block_n), lambda t: (t, 0, 0)),
            whole_spec(hat1.shape),
            whole_spec(cotangent.shape),
            whole_spec(norm_params.shape),
            whole_spec(bias_rows.shape),
        ],
        out_specs=[
            block,
            block,
            whole_spec((rows, width)),
            whole_spec((rows, width)),
            whole_spec((rows, width)),
            whole_spec((8, width)),
        ],
        out_shape=[
            struct((parts // 2, rows, 2 * block_n), bf16),
            struct((parts // 2, rows, 2 * block_n), bf16),
            struct((rows, width), bf16),
            struct((rows, width), f32),
            struct((rows, width), bf16),
            struct((8, width), f32),
        ],
        scratch_shapes=[pltpu.VMEM((rows, width), f32)],
        name="ffn",
    )(lengths, first_b, ud_all, ud_all, up_bias, hat1, cotangent, norm_params, bias_rows)


def ffn_back_kernel(
    me_ref,
    first_ref,
    g2b_ref,
    up_ref,
    down_ref,
    act_ref,
    slope_ref,
    g2_ref,
    hat_ref,
    inv_ref,
    norm_ref,
    keep_ref,
    send_ref,
    ub_ref,
    g1_ref,
    g1b_ref,
    red_ref,
    acc_ref,
    first_t_ref,
    g2_t_ref,
    grad_ref,
):
    step = pl.program_id(0)
    rows, width = first_ref.shape
    _, dp_parts, _, part_rows, block_n = up_ref.shape
    mine = me_ref[1]

    @pl.when(step == 0)
    def _():
        first_t_ref[...] = jnp.transpose(first_ref[...])
        g2_t_ref[...] = jnp.transpose(g2b_ref[...])

    grad_act = dot_nn(g2b_ref[...], joined(down_ref, width))
    grad_pre = (slope_ref[0].astype(f32) * grad_act).astype(bf16)
    ub_ref[0] = jnp.sum(grad_pre.astype(f32), axis=0, keepdims=True)
    grad_ref[0] = dot_nn(first_t_ref[...], grad_pre).astype(bf16)
    grad_ref[1] = dot_nn(g2_t_ref[...], act_ref[0]).astype(bf16)
    for slot in range(dp_parts):
        place = pl.ds(pl.multiple_of((mine ^ slot) * part_rows, 16), part_rows)
        target = send_ref if slot % 2 else keep_ref
        for which in range(2):
            for g in range(2):
                target[(me_ref[0] & 1) ^ g, slot // 2, which] = grad_ref[
                    which, place, g * block_n : (g + 1) * block_n
                ]
    piece = dot_nt(grad_pre, joined(up_ref, width))

    @pl.when(step == 0)
    def _():
        acc_ref[...] = piece

    @pl.when(step > 0)
    def _():
        acc_ref[...] += piece

    @pl.when(step == pl.num_programs(0) - 1)
    def _():
        tile = LANES
        red_ref[...] = jnp.zeros(red_ref.shape, f32)

        def one_tile(i, carry):
            place = pl.ds(pl.multiple_of(i * tile, tile), tile)
            grad = g2_ref[place, :] + acc_ref[place, :]
            hat = hat_ref[place, :]
            scaled = grad * norm_ref[0:1, :]
            g1 = inv_ref[place, :] * (
                scaled - row_mean(scaled) - hat * row_mean(scaled * hat)
            )
            g1b = g1.astype(bf16)
            g1_ref[place, :] = g1
            g1b_ref[place, :] = g1b
            red_ref[0:1, :] += jnp.sum(grad * hat, axis=0, keepdims=True)
            red_ref[1:2, :] += jnp.sum(grad, axis=0, keepdims=True)
            red_ref[2:3, :] += jnp.sum(g1b.astype(f32), axis=0, keepdims=True)
            return carry

        lax.fori_loop(0, rows // tile, one_tile, 0)


def ffn_back(me, first_b, g2b, ud_all, act, slope, g2, hat1, inv1, norm_params):
    rows, width = first_b.shape
    parts, dp_parts, _, part_rows, block_n = ud_all.shape
    weight = lambda which: pl.BlockSpec(
        (2, dp_parts, 1, part_rows, block_n), lambda t, me: (t, 0, which, 0, 0)
    )
    block = pl.BlockSpec((1, rows, 2 * block_n), lambda t, me: (t, 0, 0))
    half = pl.BlockSpec(
        (2, dp_parts // 2, 2, part_rows, block_n), lambda t, me: (t ^ (me[0] >> 1), 0, 0, 0, 0)
    )
    half_shape = struct((parts, dp_parts // 2, 2, part_rows, block_n), bf16)
    return pl.pallas_call(
        ffn_back_kernel,
        grid_spec=pltpu.PrefetchScalarGridSpec(
            num_scalar_prefetch=1,
            grid=(parts // 2,),
            in_specs=[
                whole_spec(first_b.shape),
                whole_spec(g2b.shape),
                weight(0),
                weight(1),
                block,
                block,
                whole_spec(g2.shape),
                whole_spec(hat1.shape),
                whole_spec(inv1.shape),
                whole_spec(norm_params.shape),
            ],
            out_specs=[
                half,
                half,
                pl.BlockSpec((1, 1, 2 * block_n), lambda t, me: (t, 0, 0)),
                whole_spec((rows, width)),
                whole_spec((rows, width)),
                whole_spec((8, width)),
            ],
            scratch_shapes=[
                pltpu.VMEM((rows, width), f32),
                pltpu.VMEM((width, rows), bf16),
                pltpu.VMEM((width, rows), bf16),
                pltpu.VMEM((2, width, 2 * block_n), bf16),
            ],
        ),
        out_shape=[
            half_shape,
            half_shape,
            struct((parts // 2, 1, 2 * block_n), f32),
            struct((rows, width), f32),
            struct((rows, width), bf16),
            struct((8, width), f32),
        ],
        name="ffn_back",
    )(me, first_b, g2b, ud_all, ud_all, act, slope, g2, hat1, inv1, norm_params)


def qkv_grad_kernel(me_ref, mixed_ref, ctx_ref, g1b_ref, dq_ref, dk_ref, dv_ref, dq2_ref, dk2_ref, dv2_ref, keep_ref, send_ref, gq_ref, go_ref, *, qkv_n, part_rows):
    width = mixed_ref.shape[1]
    parts = keep_ref.shape[0]
    block_n = keep_ref.shape[-1]
    out_n = block_n - qkv_n
    mixed_t = jnp.transpose(mixed_ref[...])
    for part, refs in enumerate(((dq_ref, dq2_ref), (dk_ref, dk2_ref), (dv_ref, dv2_ref))):
        right = jnp.concatenate([ref[...] for ref in refs], axis=1)
        gq_ref[:, part * width : (part + 1) * width] = dot_nn(mixed_t, right).astype(bf16)
    go_ref[...] = dot_tn(ctx_ref[...], g1b_ref[...]).astype(bf16)
    my_t = me_ref[0]
    my_d = me_ref[1]

    def one_half(s, carry):
        for core, target in ((0, keep_ref), (1, send_ref)):
            place = pl.ds(pl.multiple_of((my_d ^ (2 * s + core)) * part_rows, 16), part_rows)
            for t in range(parts):
                slot = my_t ^ t
                target[slot, s, :, :qkv_n] = gq_ref[place, t * qkv_n : (t + 1) * qkv_n]
                target[slot, s, :, qkv_n:] = go_ref[place, t * out_n : (t + 1) * out_n]
        return carry

    lax.fori_loop(0, keep_ref.shape[1], one_half, 0)


def qkv_gradient(me, mixed_b, context, g1b, heads, parts, dp_parts, qkv_n, block_n):
    rows, width = mixed_b.shape
    part_rows = width // dp_parts
    half = (parts, dp_parts // 2, part_rows, block_n)
    return pl.pallas_call(
        functools.partial(qkv_grad_kernel, qkv_n=qkv_n, part_rows=part_rows),
        grid=(1,),
        in_specs=[SMEM_SPEC] + [whole_spec((rows, width))] * 3 + [whole_spec((rows, width // 2))] * 6,
        out_specs=[whole_spec(half), whole_spec(half)],
        out_shape=[struct(half, bf16), struct(half, bf16)],
        scratch_shapes=[pltpu.VMEM((width, 3 * width), bf16), pltpu.VMEM((width, width), bf16)],
        name="qkv_gradient",
    )(me, mixed_b, context, g1b, *heads)


def tail_kernel(
    lens_ref,
    me_ref,
    dq_ref,
    dk_ref,
    dv_ref,
    dq2_ref,
    dk2_ref,
    dv2_ref,
    wqkv_ref,
    g1_ref,
    vis_ref,
    normed_ref,
    hat_ref,
    grad_ref,
    keep_ref,
    send_ref,
    red_ref,
    bn_ref,
    vgrad_ref,
    *,
    vis_n,
    groups,
):
    step = pl.program_id(0)
    tile, width = g1_ref.shape
    ends = doc_ends(lens_ref)
    grad = g1_ref[...]
    heads = [
        jnp.concatenate([a[...], b[...]], axis=1)
        for a, b in ((dq_ref, dq2_ref), (dk_ref, dk2_ref), (dv_ref, dv2_ref))
    ]
    for part, left in enumerate(heads):
        grad = grad + dot_nt(left, wqkv_ref[:, part * width : (part + 1) * width])
    grad_ref[...] = grad
    rows = lax.broadcasted_iota(jnp.int32, (tile, width), 0) + step * tile
    grad_b = jnp.where(visual_mask(rows, ends), grad, 0.0).astype(bf16)

    @pl.when(step == 0)
    def _():
        red_ref[...] = jnp.zeros(red_ref.shape, f32)
        bn_ref[...] = jnp.zeros(bn_ref.shape, f32)
        vgrad_ref[...] = jnp.zeros(vgrad_ref.shape, f32)

    vgrad_ref[...] += dot_tn(normed_ref[...], grad_b)
    back = dot_nt(grad_b, vis_ref[...])
    bn_ref[0:1, :] += jnp.sum(back * hat_ref[...], axis=0, keepdims=True)
    bn_ref[1:2, :] += jnp.sum(back, axis=0, keepdims=True)
    red_ref[0:1, :] += jnp.sum(grad_b.astype(f32), axis=0, keepdims=True)
    red_ref[1:2, :] += jnp.sum(heads[0].astype(f32), axis=0, keepdims=True)
    red_ref[2:3, :] += jnp.sum(heads[2].astype(f32), axis=0, keepdims=True)

    @pl.when(step == pl.num_programs(0) - 1)
    def _():
        parts, halves, group_rows, _ = keep_ref.shape
        my_t = me_ref[0]
        my_d = me_ref[1]
        part_rows = group_rows * groups

        def one_half(s, carry):
            for core, target in ((0, keep_ref), (1, send_ref)):
                first = (my_d ^ (2 * s + core)) * part_rows
                for g in range(groups):
                    place = pl.ds(pl.multiple_of(first + g * group_rows, 8), group_rows)
                    for t in range(parts):
                        target[my_t ^ t, s, :, g * vis_n : (g + 1) * vis_n] = vgrad_ref[
                            place, t * vis_n : (t + 1) * vis_n
                        ].astype(bf16)
            return carry

        lax.fori_loop(0, halves, one_half, 0)


def tail(lengths, me, heads, w_qkv, g1, vis_full, normed, hat_v, parts, dp_parts, block_n):
    rows, width = g1.shape
    channels = normed.shape[1]
    tile = rows // 3
    vis_n = width // parts
    groups = block_n // vis_n
    group_rows = channels // dp_parts // groups
    half = (parts, dp_parts // 2, group_rows, block_n)
    row_block = lambda n: pl.BlockSpec((tile, n), lambda i: (i, 0))
    return pl.pallas_call(
        functools.partial(tail_kernel, vis_n=vis_n, groups=groups),
        grid=(rows // tile,),
        in_specs=[
            SMEM_SPEC,
            SMEM_SPEC,
            *([row_block(width // 2)] * 6),
            whole_spec(w_qkv.shape),
            row_block(width),
            whole_spec(vis_full.shape),
            row_block(channels),
            row_block(channels),
        ],
        out_specs=[
            row_block(width),
            whole_spec(half),
            whole_spec(half),
            whole_spec((8, width)),
            whole_spec((8, channels)),
        ],
        out_shape=[
            struct((rows, width), f32),
            struct(half, bf16),
            struct(half, bf16),
            struct((8, width), f32),
            struct((8, channels), f32),
        ],
        scratch_shapes=[pltpu.VMEM((channels, width), f32)],
        name="tail",
    )(lengths, me, *heads, w_qkv, g1, vis_full, normed, hat_v)


def axis_bits(name, first=0):
    return [(name, bit) for bit in range(first, (lax.axis_size(name) - 1).bit_length())]


def flip_permute(values, axis_bit):
    name, bit = axis_bit
    return lax.ppermute(
        values, name, [(i, i ^ (1 << bit)) for i in range(lax.axis_size(name))]
    )


def butterfly_orders():
    bits = axis_bits("dp", 1) + axis_bits("tensor")
    rest, last = bits[:-1], bits[-1:]
    return [rest[shift:] + rest[:shift] + last for shift in range(3)]


class Butterfly:
    def __init__(self, keep, received, order):
        tensor_bits = (lax.axis_size("tensor") - 1).bit_length()
        dp_bits = (lax.axis_size("dp") - 1).bit_length() - 1
        dims = [2] * (tensor_bits + dp_bits) + list(keep.shape[2:])
        self.names = [("tensor", b) for b in reversed(range(tensor_bits))] + [
            ("dp", b) for b in reversed(range(1, dp_bits + 1))
        ]
        self.keep = keep.reshape(dims)
        self.received = received.reshape(dims)
        self.order = list(order)

    def total(self):
        return self.keep.astype(f32) + self.received.astype(f32)

    def sends(self):
        self.axis_bit = self.order.pop(0)
        place = self.names.index(self.axis_bit)
        self.names.pop(place)
        total = self.total().astype(bf16)
        self.keep = lax.index_in_dim(total, 0, place, keepdims=False)
        return lax.index_in_dim(total, 1, place, keepdims=False)


def beside(sums, work, anchor, extra=()):
    sending = [one.sends() for one in sums] + [value for value, _ in extra]
    bits = [one.axis_bit for one in sums] + [bit for _, bit in extra]
    sending, anchor = lax.optimization_barrier((sending, anchor))
    arrived = [flip_permute(value, bit) for value, bit in zip(sending, bits)]
    result = work(anchor)
    arrived, result = lax.optimization_barrier((arrived, result))
    for one, value in zip(sums, arrived):
        one.received = value
    return result, arrived[len(sums) :]


def spread(values):
    count = lax.axis_size("dp") * lax.axis_size("tensor")
    copies = jnp.broadcast_to(values[None], (count,) + values.shape)
    return lax.all_to_all(copies, ("dp", "tensor"), 0, 0, tiled=True)


def lamb_direction(weight, moments, gradient):
    first_moment = beta_first * moments[0] + (1.0 - beta_first) * gradient
    second_moment = beta_second * moments[1] + (1.0 - beta_second) * gradient * gradient
    direction = (
        first_moment
        / (1.0 - beta_first**STEP)
        / (jnp.sqrt(second_moment / (1.0 - beta_second**STEP)) + adam_eps)
        + weight_decay * weight
    )
    return (jnp.stack([first_moment, second_moment]), direction)


def shards(
    hidden_in,
    visual_maps,
    lengths,
    box_x,
    box_y,
    cotangent,
    vis_weight,
    vis_moments,
    qkv_weight,
    qkv_moments,
    out_weight,
    out_moments,
    up_weight,
    up_moments,
    down_weight,
    down_moments,
    up_bias,
    up_bias_moments,
    bn_params,
    bn_moments,
    norm_params,
    norm_moments,
    bias_rows,
    bias_moments,
    rel_tables,
    table_moments,
):
    rows, width = hidden_in.shape
    channels = visual_maps.shape[1]
    dp_parts = lax.axis_size("dp")
    parts = lax.axis_size("tensor")
    device_total = dp_parts * parts
    part_rows, qkv_n = qkv_weight.shape
    out_n = out_weight.shape[1]
    block_n = qkv_n + out_n
    vis_rows, vis_n = vis_weight.shape
    groups = block_n // vis_n
    group_rows = vis_rows // groups
    me = jnp.stack([lax.axis_index("tensor"), lax.axis_index("dp")]).astype(jnp.int32)
    box_x = box_x.reshape(1, rows)
    box_y = box_y.reshape(1, rows)

    vis_b = vis_weight.astype(bf16)
    qo_shard = jnp.concatenate(
        [
            jnp.concatenate([qkv_weight.astype(bf16), out_weight.astype(bf16)], axis=1),
            jnp.concatenate(
                [vis_b[g * group_rows : (g + 1) * group_rows] for g in range(groups)], axis=1
            ),
        ],
        axis=0,
    )
    qo_all = lax.all_gather(qo_shard, ("tensor", "dp"), axis=0, tiled=False).reshape(
        parts, dp_parts, part_rows + group_rows, block_n
    )
    ud_shard = jnp.stack([up_weight.astype(bf16), down_weight.astype(bf16).T])
    ud_all = lax.all_gather(ud_shard, ("tensor", "dp"), axis=0, tiled=False).reshape(
        parts, dp_parts, 2, part_rows, block_n
    )
    vis_full = (
        qo_all[:, :, part_rows:, :]
        .reshape(parts, dp_parts, group_rows, groups, vis_n)
        .transpose(1, 3, 2, 0, 4)
        .reshape(channels, width)
    )

    visual_value = visual_maps.astype(f32)
    sums = jnp.stack([jnp.sum(visual_value, axis=0), jnp.sum(visual_value * visual_value, axis=0)])
    stats = jnp.sum(spread(sums), axis=0)

    bias = relative_bias(lengths, box_x, box_y, rel_tables)
    order, spot = table_plan(box_x, box_y)
    mixed, mixed_b, projected, w_qkv, w_out, normed, hat_v = front(
        lengths,
        hidden_in,
        visual_maps,
        stats,
        bn_params,
        qo_all,
        vis_full,
        bias_rows,
        float(visual_maps.shape[0] * device_total),
        qkv_n,
        part_rows,
    )
    context, probs = attend(projected, bias, rows, width)
    first_b, hat1, inv1 = after_attention(context, mixed, w_out, bias_rows, norm_params)
    act, slope, block_out, g2, g2b, red2 = ffn(
        lengths,
        first_b,
        ud_all,
        up_bias.reshape(parts // 2, 1, 2 * block_n),
        hat1,
        cotangent,
        norm_params,
        bias_rows,
    )
    keep_ud, send_ud, up_bias_part, g1, g1b, red1 = ffn_back(
        me, first_b, g2b, ud_all, act, slope, g2, hat1, inv1, norm_params
    )
    core = ("dp", 0)
    orders = butterfly_orders()
    flat = lambda v: v.reshape(parts, dp_parts // 2, 2 * part_rows, block_n)

    def thirds(keep, received):
        count = keep.shape[2] // 3
        return [
            Butterfly(
                keep[:, :, c * count : (c + 1) * count],
                received[:, :, c * count : (c + 1) * count],
                orders[c],
            )
            for c in range(3)
        ]

    pairs = width // LANES
    grad_context, (received_ud,) = beside(
        [], lambda g: dot_nt(g, w_out).astype(bf16), g1b, [(send_ud, core)]
    )
    ud_sums = thirds(flat(keep_ud), flat(received_ud))
    back_a, _ = beside(
        ud_sums,
        lambda g: attend_back(projected, context, g, probs, 0, pairs // 2),
        grad_context,
    )
    back_b, _ = beside(
        ud_sums,
        lambda g: attend_back(projected, context, g, probs, pairs // 2, pairs // 2),
        grad_context,
    )
    heads = tuple(back_a[:3]) + tuple(back_b[:3])
    (keep_qo, send_qo), _ = beside(
        ud_sums,
        lambda h: qkv_gradient(
            me, mixed_b, context, g1b, h, parts, dp_parts, qkv_n, block_n
        ),
        heads,
    )
    rest = ud_sums if ud_sums[0].order else []
    (grad_mixed, keep_v, send_v, red3, red_bn), (received_qo,) = beside(
        rest,
        lambda h: tail(
            lengths, me, h, w_qkv, g1, vis_full, normed, hat_v, parts, dp_parts, block_n
        ),
        heads,
        [(send_qo, core)],
    )
    qo_sums = thirds(keep_qo, received_qo)
    table_parts = []
    vis_sums = []
    for part in range(4):
        source, first = ((back_a, back_b)[part // 2][3], (part % 2) * 3)
        extra = [(send_v, core)] if part == 0 else []
        sums = [one for one in ud_sums + qo_sums + vis_sums if one.order]
        made, got = beside(
            sums, lambda g: table_sums(order, spot, g, first, 3), source, extra
        )
        if part == 0:
            vis_sums = [Butterfly(keep_v, got[0], orders[1])]
        table_parts.append(made)
    while any(one.order for one in ud_sums + qo_sums + vis_sums):
        sums = [one for one in ud_sums + qo_sums + vis_sums if one.order]
        for one in sums:
            one.received = flip_permute(one.sends(), one.axis_bit)
    table_part = table_gradient(
        jnp.concatenate([made[0] for made in table_parts]),
        jnp.concatenate([made[1] for made in table_parts]),
    )
    ud_grad = jnp.concatenate([one.total() for one in ud_sums], axis=0)
    up_shard = ud_grad[:part_rows]
    down_shard = ud_grad[part_rows:].T
    qo_grad = jnp.concatenate([one.total() for one in qo_sums], axis=0)
    qkv_shard, out_shard = qo_grad[:, :qkv_n], qo_grad[:, qkv_n:]
    vis_piece = vis_sums[0].total()
    vis_shard = jnp.concatenate(
        [vis_piece[:, g * vis_n : (g + 1) * vis_n] for g in range(groups)], axis=0
    )

    small = [
        up_bias_part.reshape(-1),
        red_bn[0:2].reshape(-1),
        jnp.concatenate([red1[0:2], red2[0:2]]).reshape(-1),
        jnp.concatenate([red3[0:3], red1[2:3], red2[2:3]]).reshape(-1),
        table_part.reshape(-1),
    ]
    small_shapes = [
        up_bias.shape,
        bn_params.shape,
        norm_params.shape,
        bias_rows.shape,
        rel_tables.shape,
    ]
    sizes = [piece.shape[0] for piece in small]
    piece_n = -(-sum(sizes) // device_total)
    padding = jnp.zeros((piece_n * device_total - sum(sizes),), f32)
    packed = jnp.concatenate(small + [padding]).reshape(device_total, piece_n)
    own_piece = jnp.sum(
        lax.all_to_all(packed, ("dp", "tensor"), 0, 0, tiled=True), axis=0
    )

    sharded = [
        (vis_weight, vis_moments, vis_shard),
        (qkv_weight, qkv_moments, qkv_shard),
        (out_weight, out_moments, out_shard),
        (up_weight, up_moments, up_shard),
        (down_weight, down_moments, down_shard),
    ]
    sharded_updates = [lamb_direction(triple[0], triple[1], triple[2]) for triple in sharded]
    local_sums = jnp.stack(
        [jnp.sum(triple[0] * triple[0]) for triple in sharded]
        + [jnp.sum(update[1] * update[1]) for update in sharded_updates]
    )
    shared = spread(jnp.concatenate([own_piece, local_sums]))
    totals = shared[:, :piece_n].reshape(-1)
    global_sums = jnp.sum(shared[:, piece_n:], axis=0).reshape(2, 5)
    small_grads = []
    start = 0
    for size, shape in zip(sizes, small_shapes):
        small_grads.append(totals[start : start + size].reshape(shape))
        start += size
    whole = [
        (up_bias, up_bias_moments, small_grads[0]),
        (bn_params, bn_moments, small_grads[1]),
        (norm_params, norm_moments, small_grads[2]),
        (bias_rows, bias_moments, small_grads[3]),
        (rel_tables, table_moments, small_grads[4]),
    ]
    whole_updates = [lamb_direction(triple[0], triple[1], triple[2]) for triple in whole]
    whole_sums = jnp.stack(
        [
            jnp.stack([jnp.sum(triple[0] * triple[0]) for triple in whole]),
            jnp.stack([jnp.sum(update[1] * update[1]) for update in whole_updates]),
        ]
    )
    all_sums = jnp.concatenate([global_sums, whole_sums], axis=1)
    weight_norms = jnp.sqrt(all_sums[0])
    update_norms = jnp.sqrt(all_sums[1])
    trust_ratio = weight_norms / update_norms
    lamb_norms = jnp.stack([weight_norms, update_norms, trust_ratio])
    outputs = [block_out, grad_mixed, lamb_norms]
    triples = sharded + whole
    updates = sharded_updates + whole_updates
    for number in range(10):
        new_weight = triples[number][0] - learn_rate * trust_ratio[number] * updates[number][1]
        outputs.extend(
            [triples[number][2], new_weight, updates[number][0], new_weight.astype(bf16)]
        )
    return tuple(outputs)


def solution(mesh):
    in_specs = (
        P(("dp", "tensor"), None),
        P(("dp", "tensor"), None),
        P(("dp", "tensor"), None),
        P(("dp", "tensor")),
        P(("dp", "tensor")),
        P(("dp", "tensor"), None),
        P("dp", "tensor"),
        P(None, "dp", "tensor"),
        P("dp", "tensor"),
        P(None, "dp", "tensor"),
        P("dp", "tensor"),
        P(None, "dp", "tensor"),
        P("dp", "tensor"),
        P(None, "dp", "tensor"),
        P("tensor", "dp"),
        P(None, "tensor", "dp"),
        P(),
        P(),
        P(),
        P(),
        P(),
        P(),
        P(),
        P(),
        P(),
        P(),
    )
    out_specs = (
        P(("dp", "tensor"), None),
        P(("dp", "tensor"), None),
        P(),
        P("dp", "tensor"),
        P("dp", "tensor"),
        P(None, "dp", "tensor"),
        P("dp", "tensor"),
        P("dp", "tensor"),
        P("dp", "tensor"),
        P(None, "dp", "tensor"),
        P("dp", "tensor"),
        P("dp", "tensor"),
        P("dp", "tensor"),
        P(None, "dp", "tensor"),
        P("dp", "tensor"),
        P("dp", "tensor"),
        P("dp", "tensor"),
        P(None, "dp", "tensor"),
        P("dp", "tensor"),
        P("tensor", "dp"),
        P("tensor", "dp"),
        P(None, "tensor", "dp"),
        P("tensor", "dp"),
        P(),
        P(),
        P(),
        P(),
        P(),
        P(),
        P(),
        P(),
        P(),
        P(),
        P(),
        P(),
        P(),
        P(),
        P(),
        P(),
        P(),
        P(),
        P(),
        P(),
    )
    return jax.shard_map(shards, mesh=mesh, in_specs=in_specs, out_specs=out_specs, check_vma=False)
```

time: 1630 us -> 506 us (0.31)
  waiting for transfers between devices: 602 us -> 20.3 us
  matrix products: 479 us -> 4.18 us
  Pallas kernels: 0 us -> 306 us
  local copies, waits for them, and re-layouts: 226 us -> 48.5 us
  blocking collectives: 150 us -> 0 us
  loops' own time: 47 us -> 0 us
  starting transfers between devices: 0.75 us -> 47.4 us
  other arithmetic: 91.6 us -> 48.6 us
    dot_general x44 -> x3, matrix products: 454 us -> 4.18 us  [the longest x1 3.54 us: dot_nt(): lax.dot_general(left, right, (((1,), (1,)), ((), ())), preferred_element_...]
    pallas_call x0 -> x15, Pallas kernels: none -> 306 us  [the longest x1 99.4 us: relative_bias(): pl.pallas_call(bias_kernel, grid=(rows // tile,), in_specs=[SMEM_SPEC, wh...]
    reduce_scatter x7 -> x0, waiting for transfers between devices: 293 us -> none  [the longest x1 159 us: shards(): lax.psum_scatter(jnp.dot(lax.slice_in_dim(act_b, 0, row_count * lax.axis_...]
    all_gather x4 -> x2, waiting for transfers between devices: 257 us -> 0.01 us  [the longest x1 0.01 us: shards(): lax.all_gather(ud_shard, ('tensor', 'dp'), axis=0, tiled=False)]
    psum x2 -> x0, blocking collectives: 80.1 us -> none  [the longest x1 41.1 us: shards(): lax.psum((up_bias_grad, bn_grad, norm_grad, bias_grad, table_grad), ('dp'...]
    all_gather x6 -> x0, blocking collectives: 69.6 us -> none  [the longest x1 33.5 us: shards(): lax.all_gather(vis_cols, 'tensor', axis=1, tiled=True)]
    dynamic_slice x73 -> x0, local copies, waits for them, and re-layouts: 64.7 us -> none  [the longest x48 49.3 us: one_hot_block(): lax.dynamic_slice_in_dim(ids, start, span_rows, 0)[:, :, None] == columns]
    unnamed x17 -> x2, waiting for transfers between devices: 52.4 us -> 0.03 us
  transfers between devices with their start and end apart: 14 -> 36, of which waited for: 7 -> 6; matrix products, arithmetic and copies ran while one was open for 42% -> 7% of each run, Pallas kernels for 0% -> 52%
where the time goes in v1:
time: 506 us; the launch traced here: 497 us
  Pallas kernels  306 us (60%)
  other arithmetic  48.6 us (10%)
  local copies, waits for them, and re-layouts  48.5 us (10%)
  starting transfers between devices  47.4 us (9%)
  between operations  22.5 us (4%)
  waiting for transfers between devices  20.3 us (4%)
    pallas_call x1, Pallas kernels, relative_bias(): pl.pallas_call(bias_kernel, grid=(rows // tile,), in_specs=[SMEM_SPEC, wh...  99.4 us
    pallas_call x4, Pallas kernels, table_sums(): pl.pallas_call(table_kernel, grid=(heads,), in_specs=[whole_spec(order.sh...  54.7 us
    ppermute x31, starting transfers between devices, flip_permute(): lax.ppermute(values, name, [(i, i ^ 1 << bit) for i in range(lax.axis_siz...  34.5 us
    pallas_call x1, Pallas kernels, attend(): pl.pallas_call(attend_kernel, grid=(pairs, rows // tile), in_specs=[pl.Bl...  30.7 us
    pallas_call x1, Pallas kernels, ffn_back(): pl.pallas_call(ffn_back_kernel, grid_spec=pltpu.PrefetchScalarGridSpec(nu...  27.9 us
    pallas_call x2, Pallas kernels, attend_back(): pl.pallas_call(attend_back_kernel, grid=(n,), in_specs=[column(0), column...  26.2 us
    pallas_call x1, Pallas kernels, ffn(): pl.pallas_call(ffn_kernel, grid=(parts // 2,), in_specs=[SMEM_SPEC, whole...  19.7 us
    unnamed x165, local copies, waits for them, and re-layouts  14.1 us
  transfers between devices with their start and end apart: 36, of which 6 were waited for; matrix products, arithmetic and copies ran while one was open for 7% of the time, Pallas kernels for 52%

profile of v1, /device:TPU:0, one launch (start us, length us, event | category | flops | bytes accessed | tf_op | source)
XLA Modules:
  0.0 496.9 jit_solution(1791470683232164740)
XLA Ops:
  13.4 7.3 %all-to-all-start = ((f32[32,2,256]{2,1,0:T(2,128)}), f32[32,2,256]{2,1,0:T(2,128)S(1)}, u32[]{:S(2)}, u32[]{:S(2)}) async-start(f32[32,2,256]{2,1,0:T(2,128)} %broadcast_in_dim.10), calls=%async_computation | async-start | bytes 131072 | tf_op jit(solution)/shard_map/all_to_all | solution.py:1052
  21.9 99.4 %relative_bias.1.bias_ref = f32[12,768,768]{2,1,0:T(8,128)} custom-call(s32[1,3]{1,0:T(1,128)} %lens_ref.7, s32[1,768]{1,0:T(1,128)} %reshape.646.xs_ref.xt_ref, s32[1,768]{1,0:T(1,128)} %reshape.647.ys_ref.yt_ref, s32[1,768]{1,0:T(1,128)} %reshape.646.xs_ref.xt_ref, s32[1,768]{1,0:T(1,128)} %reshape.647.ys_ref.yt_ref, f32[12,160]{1,0:T(8,128)} %tab_ref.1), custom_call_target="tpu_custom_call" | custom-call | tf_op jit(solution)/shard_map/relative_bias/pallas_call | solution.py:164
  125.4 11.3 %front.1 = (f32[768,768]{1,0:T(8,128)}, bf16[768,768]{1,0:T(8,128)(2,1)}, bf16[768,2304]{1,0:T(8,128)(2,1)}, bf16[768,2304]{1,0:T(8,128)(2,1)}, bf16[768,768]{1,...) custom-call(s32[1,3]{1,0:T(1,128)} %lens_ref.7, bf16[768,768]{1,0:T(8,128)(2,1)} %hidden_ref.1, ...), custom_call_target="tpu_custom_call" | custom-call | tf_op jit(solution)/shard_map/front/pallas_call | solution.py:260
  136.7 30.7 %attend.1 = (bf16[768,768]{1,0:T(8,128)(2,1)}, bf16[12,768,768]{2,1,0:T(8,128)(2,1)}) custom-call(bf16[768,2304]{1,0:T(8,128)(2,1)} %get-tuple-element.195.q_ref.k_ref.v_ref, bf16[768,2304]{1,0:T(8,128)(2,1)} %get-tuple-element.195.q_ref.k_ref.v_ref, bf16[768,2304]{1,0:T(8,128)(2,1)} %get-tuple-element.195.q_ref.k_ref.v_ref, ...), custom_call_target="tpu_custom_call" | custom-call | tf_op jit(solution)/shard_map/attend/pallas_call | solution.py:320
  167.4 6.1 %after_attention.1 = (bf16[768,768]{1,0:T(8,128)(2,1)}, f32[768,768]{1,0:T(8,128)}, f32[768,1]{1,0:T(8,128)}) custom-call(bf16[768,768]{1,0:T(8,128)(2,1)} %get-tuple-element.196.ctx_ref, f32[768,768]{1,0:T(8,128)} %get-tuple-element.197.mixed_ref, bf16[768,768]{1,0:T(8,128)(2,1)} %get-tuple-element.198.wout_ref, f32[5,768]{1,0:T(8,128)} %bias_ref.5, ...), custom_call_target="tpu_custom_call" | custom-call | tf_op jit(solution)/shard_map/after_attention/pallas_call | solution.py:570
  173.5 19.7 %ffn.1 = (bf16[4,768,768]{2,1,0:T(8,128)(2,1)}, bf16[4,768,768]{2,1,0:T(8,128)(2,1)}, bf16[768,768]{1,0:T(8,128)(2,1)}, f32[768,768]{1,0:T(8,128)}, bf16[768,768]{1,0:T(8,128)(2,1)}, /*index=5*/f32[8,768]{1,0:T(8,128)}) custom-call(s32[1,3]{1,0:T(1,128)} %lens_ref.7, bf16[768,768]{1,0:T(8,128)(2,1)} %get-tuple-element.199.first_ref, ...), custom_call_target="tpu_custom_call" | custom-call | tf_op jit(solution)/shard_map/ffn/pallas_call | solution.py:672
  193.3 27.9 %ffn_back.1 = (bf16[8,2,2,192,384]{4,3,2,1,0:T(8,128)(2,1)}, bf16[8,2,2,192,384]{4,3,2,1,0:T(8,128)(2,1)}, f32[4,1,768]{2,1,0:T(1,128)}, f32[768,768]{1,0:T(8,12...) custom-call(s32[2]{0:T(128)} %pad_add_fusion.me_ref, bf16[768,768]{1,0:T(8,128)(2,1)} %get-tuple-element.199.first_ref, ...), custom_call_target="tpu_custom_call" | custom-call | tf_op jit(solution)/shard_map/ffn_back/pallas_call | solution.py:798
  221.4 3.5 convolution_convert_fusion.gctx_ref
  224.9 4.5 collective-permute-done
  238.7 12.9 %attend_back.2 = (bf16[768,384]{1,0:T(8,128)(2,1)}, bf16[768,384]{1,0:T(8,128)(2,1)}, bf16[768,384]{1,0:T(8,128)(2,1)}, bf16[6,768,768]{2,1,0:T(8,128)(2,1)}) custom-call(bf16[768,2304]{1,0:T(8,128)(2,1)} %get-tuple-element.195.q_ref.k_ref.v_ref, bf16[768,2304]{1,0:T(8,128)(2,1)} %get-tuple-element.195.q_ref.k_ref.v_ref, ...), custom_call_target="tpu_custom_call" | custom-call | tf_op jit(solution)/shard_map/attend_back/pallas_call | solution.py:380
  265.8 13.3 %attend_back.3 = (bf16[768,384]{1,0:T(8,128)(2,1)}, bf16[768,384]{1,0:T(8,128)(2,1)}, bf16[768,384]{1,0:T(8,128)(2,1)}, bf16[6,768,768]{2,1,0:T(8,128)(2,1)}) custom-call(bf16[768,2304]{1,0:T(8,128)(2,1)} %get-tuple-element.195.q_ref.k_ref.v_ref, bf16[768,2304]{1,0:T(8,128)(2,1)} %get-tuple-element.195.q_ref.k_ref.v_ref, ...), custom_call_target="tpu_custom_call" | custom-call | tf_op jit(solution)/shard_map/attend_back/pallas_call | solution.py:380
  284.7 10.8 %qkv_gradient.1 = (bf16[8,2,192,384]{3,2,1,0:T(8,128)(2,1)}, bf16[8,2,192,384]{3,2,1,0:T(8,128)(2,1)}) custom-call(s32[2]{0:T(128)} %pad_add_fusion.me_ref, bf16[768,768]{1,0:T(8,128)(2,1)} %get-tuple-element.246.mixed_ref, bf16[768,768]{1,0:T(8,128)(2,1)} %get-tuple-element.196.ctx_ref, bf16[768,768]{1,0:T(8,128)(2,1)} %get-tuple-element.211.g1b_ref, ...), custom_call_target="tpu_custom_call" | custom-call | tf_op jit(solution)/shard_map/qkv_gradient/pallas_call | solution.py:871
  295.9 7.8 %table_plan.1 = (bf16[768,1536]{1,0:T(8,128)(2,1)}, s32[768,128]{1,0:T(8,128)}) custom-call(s32[1,768]{1,0:T(1,128)} %reshape.646.xs_ref.xt_ref, s32[1,768]{1,0:T(1,128)} %reshape.647.ys_ref.yt_ref, s32[1,128]{1,0:T(1,128)} %constant.68.clone.theta_ref), custom_call_target="tpu_custom_call" | custom-call | tf_op jit(solution)/shard_map/table_plan/pallas_call | solution.py:474
  316.8 10.8 %tail.1 = (f32[768,768]{1,0:T(8,128)}, bf16[8,2,16,384]{3,2,1,0:T(8,128)(2,1)}, bf16[8,2,16,384]{3,2,1,0:T(8,128)(2,1)}, f32[8,768]{1,0:T(8,128)}, f32[8,256]{1,0:T(8,128)}) custom-call(s32[1,3]{1,0:T(1,128)} %lens_ref.7, s32[2]{0:T(128)} %pad_add_fusion.me_ref, bf16[768,384]{1,0:T(8,128)(2,1)} %get-tuple-element.263.dq_ref, ...), custom_call_target="tpu_custom_call" | custom-call | tf_op jit(solution)/shard_map/tail/pallas_call | solution.py:964
  342.0 13.8 %table_sums.4 = (f32[3,8,128]{2,1,0:T(8,128)}, f32[3,8,1536]{2,1,0:T(8,128)}) custom-call(bf16[768,1536]{1,0:T(8,128)(2,1)} %get-tuple-element.292.order_ref, s32[768,128]{1,0:T(8,128)} %get-tuple-element.293.spot_ref, bf16[6,768,768]{2,1,0:T(8,128)(2,1)} %get-tuple-element.307.gs_ref), custom_call_target="tpu_custom_call" | custom-call | tf_op jit(solution)/shard_map/table_sums/pallas_call | solution.py:518
  368.9 13.6 %table_sums.5 = (f32[3,8,128]{2,1,0:T(8,128)}, f32[3,8,1536]{2,1,0:T(8,128)}) custom-call(bf16[768,1536]{1,0:T(8,128)(2,1)} %get-tuple-element.292.order_ref, s32[768,128]{1,0:T(8,128)} %get-tuple-element.293.spot_ref, bf16[6,768,768]{2,1,0:T(8,128)(2,1)} %get-tuple-element.307.gs_ref), custom_call_target="tpu_custom_call" | custom-call | tf_op jit(solution)/shard_map/table_sums/pallas_call | solution.py:518
  389.7 13.6 %table_sums.6 = (f32[3,8,128]{2,1,0:T(8,128)}, f32[3,8,1536]{2,1,0:T(8,128)}) custom-call(bf16[768,1536]{1,0:T(8,128)(2,1)} %get-tuple-element.292.order_ref, s32[768,128]{1,0:T(8,128)} %get-tuple-element.293.spot_ref, bf16[6,768,768]{2,1,0:T(8,128)(2,1)} %get-tuple-element.332.gs_ref), custom_call_target="tpu_custom_call" | custom-call | tf_op jit(solution)/shard_map/table_sums/pallas_call | solution.py:518
  410.4 13.8 %table_sums.7 = (f32[3,8,128]{2,1,0:T(8,128)}, f32[3,8,1536]{2,1,0:T(8,128)}) custom-call(bf16[768,1536]{1,0:T(8,128)(2,1)} %get-tuple-element.292.order_ref, s32[768,128]{1,0:T(8,128)} %get-tuple-element.293.spot_ref, bf16[6,768,768]{2,1,0:T(8,128)(2,1)} %get-tuple-element.332.gs_ref), custom_call_target="tpu_custom_call" | custom-call | tf_op jit(solution)/shard_map/table_sums/pallas_call | solution.py:518
  433.6 2.9 all-to-all-start.1
  439.5 4.3 all-to-all-done.1
  443.8 6.6 %concatenate.89 = f32[398]{0:T(512)S(1)} concatenate(f32[388]{0:T(512)S(1)} %reduce_sum.248, f32[1]{0:T(128)} %bitcast.68, f32[1]{0:T(128)} %bitcast.69, f32[1]{0:T(128)} %bitcast.70, f32[1]{0:T(128)} %bitcast.71, f32[1]{0:T(128)} %bitcast.72, f32[1]{0:T(128)} %bitcast.78, f32[1]{0:T(128)} %bitcast.84, f32[1]{0:T(128)} %bitcast.87, f32[1]{0:T(128)} %bitcast.92, f32[1]{0:T(128)} %bitcast.97), dimensions={0} | concatenate | bytes 3184 | tf_op jit(solution)/shard_map/concatenate | solution.py:1280
  454.2 6.6 %all-to-all-done.2 = f32[32,1,398]{2,1,0:T(1,128)S(1)} async-done(((f32[32,1,398]{2,1,0:T(1,128)}), f32[32,1,398]{2,1,0:T(1,128)S(1)}, u32[]{:S(2)}, u32[]{:S(2)}) %all-to-all-start.2) | async-done | bytes 50976 | tf_op jit(solution)/shard_map/all_to_all | solution.py:1052
  465.9 3.3 stack.202
  469.3 3.3 stack.209
  (393 shorter events, 126.6 us)
Async XLA Ops:
  7.2 115.2 %all-gather.5.cloned.1.call-start = ((), (), s32[]{:S(2)}) async-start(), calls=%async_computation.3 | async-start | bytes 5271552 | tf_op jit(solution)/shard_map/all_gather | solution.py:1120
  10.8 162.7 %all-gather.7.cloned.1.call-start = ((), (), s32[]{:S(2)}) async-start(), calls=%async_computation.4 | async-start | bytes 9732096 | tf_op jit(solution)/shard_map/all_gather | solution.py:1124
  13.4 108.5 %all-to-all-start = ((f32[32,2,256]{2,1,0:T(2,128)}), f32[32,2,256]{2,1,0:T(2,128)S(1)}, u32[]{:S(2)}, u32[]{:S(2)}) async-start(f32[32,2,256]{2,1,0:T(2,128)} %broadcast_in_dim.10), calls=%async_computation | async-start | bytes 131072 | tf_op jit(solution)/shard_map/all_to_all | solution.py:1052
  234.2 19.9 %collective-permute-start.1 = (bf16[2,2,2,128,384]{4,3,2,1,0:T(8,128)(2,1)}, bf16[2,2,2,128,384]{4,3,2,1,0:T(8,128)(2,1)}, u32[]{:S(2)}, u32[]{:S(2)}) collective-permute-start(bf16[2,2,2,128,384]{4,3,2,1,0:T(8,128)(2,1)} %slice_bitcast_fusion), channel_id=1, source_target_pairs={{0,16},{8,24},{16,0},{24,8},{1,17},{9,25},{17,1},{25,9},{2,18},{10... | collective-permute-start | bytes 2359304 | tf_op jit(solution)/shard_map/ppermute | solution.py:1002
  235.9 19.6 %collective-permute-start.2 = (bf16[2,2,2,128,384]{4,3,0,2,1:T(8,128)(2,1)}, bf16[2,2,2,128,384]{4,3,0,2,1:T(8,128)(2,1)}, u32[]{:S(2)}, u32[]{:S(2)}) collective-permute-start(bf16[2,2,2,128,384]{4,3,0,2,1:T(8,128)(2,1)} %bitcast.429), channel_id=1, source_target_pairs={{0,1},{1,0},{2,3},{3,2},{4,5},{5,4},{6,7},{7,6},{8,9},{9,8},{10,11... | collective-permute-start | bytes 2359304 | tf_op jit(solution)/shard_map/ppermute | solution.py:1002
  237.3 19.1 %collective-permute-start.3 = (bf16[2,2,2,128,384]{4,3,0,1,2:T(8,128)(2,1)S(1)}, bf16[2,2,2,128,384]{4,3,0,1,2:T(8,128)(2,1)}, u32[]{:S(2)}, u32[]{:S(2)}) collective-permute-start(bf16[2,2,2,128,384]{4,3,0,1,2:T(8,128)(2,1)S(1)} %bitcast.453), channel_id=1, source_target_pairs={{0,2},{1,3},{2,0},{3,1},{4,6},{5,7},{6,4},{7,5},{8,10},{9,11},{10,... | collective-permute-start | bytes 2359304 | tf_op jit(solution)/shard_map/ppermute | solution.py:1002
  263.0 16.1 %collective-permute-start.4 = (bf16[2,2,128,384]{3,2,1,0:T(8,128)(2,1)S(1)}, bf16[2,2,128,384]{3,2,1,0:T(8,128)(2,1)S(1)}, u32[]{:S(2)}, u32[]{:S(2)}) collective-permute-start(bf16[2,2,128,384]{3,2,1,0:T(8,128)(2,1)S(1)} %slice_bitcast_fusion.6), channel_id=1, source_target_pairs={{0,1},{1,0},{2,3},{3,2},{4,5},{5,4},{6,7},{7,6},{8,9},{9,8},{10,11... | collective-permute-start | bytes 1179656 | tf_op jit(solution)/shard_map/ppermute | solution.py:1002
  295.8 32.0 %collective-permute-start.13 = (bf16[8,2,192,384]{3,2,1,0:T(8,128)(2,1)}, bf16[8,2,192,384]{3,2,1,0:T(8,128)(2,1)}, u32[]{:S(2)}, u32[]{:S(2)}) collective-permute-start(bf16[8,2,192,384]{3,2,1,0:T(8,128)(2,1)} %get-tuple-element.262), channel_id=1, source_target_pairs={{0,8},{8,0},{16,24},{24,16},{1,9},{9,1},{17,25},{25,17},{2,10},{10... | collective-permute-start | bytes 7077896 | tf_op jit(solution)/shard_map/ppermute | solution.py:1002
  310.9 16.8 %collective-permute-start.10 = (bf16[128,384]{1,0:T(8,128)(2,1)S(1)}, bf16[128,384]{1,0:T(8,128)(2,1)S(1)}, u32[]{:S(2)}, u32[]{:S(2)}) collective-permute-start(bf16[128,384]{1,0:T(8,128)(2,1)S(1)} %slice_bitcast_fusion.31), channel_id=1, source_target_pairs={{0,4},{1,5},{2,6},{3,7},{4,0},{5,1},{6,2},{7,3},{8,12},{9,13},{10,... | collective-permute-start | bytes 294920 | tf_op jit(solution)/shard_map/ppermute | solution.py:1002
  337.2 21.3 %collective-permute-start.14 = (bf16[2,2,2,64,384]{4,3,0,1,2:T(8,128)(2,1)}, bf16[2,2,2,64,384]{4,3,0,1,2:T(8,128)(2,1)}, u32[]{:S(2)}, u32[]{:S(2)}) collective-permute-start(bf16[2,2,2,64,384]{4,3,0,1,2:T(8,128)(2,1)} %bitcast.433), channel_id=1, source_target_pairs={{0,16},{8,24},{16,0},{24,8},{1,17},{9,25},{17,1},{25,9},{2,18},{10... | collective-permute-start | bytes 1179656 | tf_op jit(solution)/shard_map/ppermute | solution.py:1002
  337.8 20.7 %collective-permute-start.15 = (bf16[2,2,2,64,384]{4,3,0,2,1:T(8,128)(2,1)}, bf16[2,2,2,64,384]{4,3,0,2,1:T(8,128)(2,1)}, u32[]{:S(2)}, u32[]{:S(2)}) collective-permute-start(bf16[2,2,2,64,384]{4,3,0,2,1:T(8,128)(2,1)} %bitcast.432), channel_id=1, source_target_pairs={{0,1},{1,0},{2,3},{3,2},{4,5},{5,4},{6,7},{7,6},{8,9},{9,8},{10,11... | collective-permute-start | bytes 1179656 | tf_op jit(solution)/shard_map/ppermute | solution.py:1002
  338.4 20.1 %collective-permute-start.16 = (bf16[2,2,2,64,384]{4,3,0,1,2:T(8,128)(2,1)}, bf16[2,2,2,64,384]{4,3,0,1,2:T(8,128)(2,1)}, u32[]{:S(2)}, u32[]{:S(2)}) collective-permute-start(bf16[2,2,2,64,384]{4,3,0,1,2:T(8,128)(2,1)} %bitcast.431), channel_id=1, source_target_pairs={{0,2},{1,3},{2,0},{3,1},{4,6},{5,7},{6,4},{7,5},{8,10},{9,11},{10,... | collective-permute-start | bytes 1179656 | tf_op jit(solution)/shard_map/ppermute | solution.py:1002
  339.9 18.6 %collective-permute-start.17 = (bf16[8,2,16,384]{3,2,1,0:T(8,128)(2,1)}, bf16[8,2,16,384]{3,2,1,0:T(8,128)(2,1)}, u32[]{:S(2)}, u32[]{:S(2)}) collective-permute-start(bf16[8,2,16,384]{3,2,1,0:T(8,128)(2,1)} %get-tuple-element.291), channel_id=1, source_target_pairs={{0,8},{8,0},{16,24},{24,16},{1,9},{9,1},{17,25},{25,17},{2,10},{10... | collective-permute-start | bytes 589832 | tf_op jit(solution)/shard_map/ppermute | solution.py:1002
  363.0 19.5 %collective-permute-start.18 = (bf16[2,2,64,384]{3,2,0,1:T(8,128)(2,1)S(1)}, bf16[2,2,64,384]{3,2,0,1:T(8,128)(2,1)S(1)}, u32[]{:S(2)}, u32[]{:S(2)}) collective-permute-start(bf16[2,2,64,384]{3,2,0,1:T(8,128)(2,1)S(1)} %slice_bitcast_fusion.13), channel_id=1, source_target_pairs={{0,1},{1,0},{2,3},{3,2},{4,5},{5,4},{6,7},{7,6},{8,9},{9,8},{10,11... | collective-permute-start | bytes 589832 | tf_op jit(solution)/shard_map/ppermute | solution.py:1002
  364.6 17.9 %collective-permute-start.19 = (bf16[2,2,64,384]{3,2,0,1:T(8,128)(2,1)S(1)}, bf16[2,2,64,384]{3,2,0,1:T(8,128)(2,1)S(1)}, u32[]{:S(2)}, u32[]{:S(2)}) collective-permute-start(bf16[2,2,64,384]{3,2,0,1:T(8,128)(2,1)S(1)} %slice_bitcast_fusion.12), channel_id=1, source_target_pairs={{0,2},{1,3},{2,0},{3,1},{4,6},{5,7},{6,4},{7,5},{8,10},{9,11},{10,... | collective-permute-start | bytes 589832 | tf_op jit(solution)/shard_map/ppermute | solution.py:1002
  365.0 17.5 %collective-permute-start.20 = (bf16[2,2,64,384]{3,2,0,1:T(8,128)(2,1)S(1)}, bf16[2,2,64,384]{3,2,0,1:T(8,128)(2,1)S(1)}, u32[]{:S(2)}, u32[]{:S(2)}) collective-permute-start(bf16[2,2,64,384]{3,2,0,1:T(8,128)(2,1)S(1)} %slice_bitcast_fusion.11), channel_id=1, source_target_pairs={{0,16},{8,24},{16,0},{24,8},{1,17},{9,25},{17,1},{25,9},{2,18},{10... | collective-permute-start | bytes 589832 | tf_op jit(solution)/shard_map/ppermute | solution.py:1002
  383.4 19.8 %collective-permute-start.22 = (bf16[2,64,384]{2,1,0:T(8,128)(2,1)S(1)}, bf16[2,64,384]{2,1,0:T(8,128)(2,1)S(1)}, u32[]{:S(2)}, u32[]{:S(2)}) collective-permute-start(bf16[2,64,384]{2,1,0:T(8,128)(2,1)S(1)} %slice_bitcast_fusion.28), channel_id=1, source_target_pairs={{0,2},{1,3},{2,0},{3,1},{4,6},{5,7},{6,4},{7,5},{8,10},{9,11},{10,... | collective-permute-start | bytes 294920 | tf_op jit(solution)/shard_map/ppermute | solution.py:1002
  385.1 18.1 %collective-permute-start.23 = (bf16[2,64,384]{2,1,0:T(8,128)(2,1)S(1)}, bf16[2,64,384]{2,1,0:T(8,128)(2,1)S(1)}, u32[]{:S(2)}, u32[]{:S(2)}) collective-permute-start(bf16[2,64,384]{2,1,0:T(8,128)(2,1)S(1)} %slice_bitcast_fusion.27), channel_id=1, source_target_pairs={{0,16},{8,24},{16,0},{24,8},{1,17},{9,25},{17,1},{25,9},{2,18},{10... | collective-permute-start | bytes 294920 | tf_op jit(solution)/shard_map/ppermute | solution.py:1002
  385.6 17.6 %collective-permute-start.24 = (bf16[2,64,384]{2,1,0:T(8,128)(2,1)S(1)}, bf16[2,64,384]{2,1,0:T(8,128)(2,1)S(1)}, u32[]{:S(2)}, u32[]{:S(2)}) collective-permute-start(bf16[2,64,384]{2,1,0:T(8,128)(2,1)S(1)} %slice_bitcast_fusion.26), channel_id=1, source_target_pairs={{0,1},{1,0},{2,3},{3,2},{4,5},{5,4},{6,7},{7,6},{8,9},{9,8},{10,11... | collective-permute-start | bytes 294920 | tf_op jit(solution)/shard_map/ppermute | solution.py:1002
  387.2 16.1 %collective-permute-start.25 = (bf16[2,2,16,384]{3,2,0,1:T(8,128)(2,1)}, bf16[2,2,16,384]{3,2,0,1:T(8,128)(2,1)S(1)}, u32[]{:S(2)}, u32[]{:S(2)}) collective-permute-start(bf16[2,2,16,384]{3,2,0,1:T(8,128)(2,1)} %slice_bitcast_fusion.39), channel_id=1, source_target_pairs={{0,2},{1,3},{2,0},{3,1},{4,6},{5,7},{6,4},{7,5},{8,10},{9,11},{10,... | collective-permute-start | bytes 147464 | tf_op jit(solution)/shard_map/ppermute | solution.py:1002
  403.5 20.8 %collective-permute-start.26 = (bf16[64,384]{1,0:T(8,128)(2,1)S(1)}, bf16[64,384]{1,0:T(8,128)(2,1)S(1)}, u32[]{:S(2)}, u32[]{:S(2)}) collective-permute-start(bf16[64,384]{1,0:T(8,128)(2,1)S(1)} %slice_bitcast_fusion.38), channel_id=1, source_target_pairs={{0,4},{1,5},{2,6},{3,7},{4,0},{5,1},{6,2},{7,3},{8,12},{9,13},{10,... | collective-permute-start | bytes 147464 | tf_op jit(solution)/shard_map/ppermute | solution.py:1002
  404.7 19.6 %collective-permute-start.27 = (bf16[64,384]{1,0:T(8,128)(2,1)S(1)}, bf16[64,384]{1,0:T(8,128)(2,1)S(1)}, u32[]{:S(2)}, u32[]{:S(2)}) collective-permute-start(bf16[64,384]{1,0:T(8,128)(2,1)S(1)} %slice_bitcast_fusion.37), channel_id=1, source_target_pairs={{0,4},{1,5},{2,6},{3,7},{4,0},{5,1},{6,2},{7,3},{8,12},{9,13},{10,... | collective-permute-start | bytes 147464 | tf_op jit(solution)/shard_map/ppermute | solution.py:1002
  406.5 17.8 %collective-permute-start.28 = (bf16[64,384]{1,0:T(8,128)(2,1)S(1)}, bf16[64,384]{1,0:T(8,128)(2,1)S(1)}, u32[]{:S(2)}, u32[]{:S(2)}) collective-permute-start(bf16[64,384]{1,0:T(8,128)(2,1)S(1)} %slice_bitcast_fusion.36), channel_id=1, source_target_pairs={{0,4},{1,5},{2,6},{3,7},{4,0},{5,1},{6,2},{7,3},{8,12},{9,13},{10,... | collective-permute-start | bytes 147464 | tf_op jit(solution)/shard_map/ppermute | solution.py:1002
  407.6 16.6 %collective-permute-start.29 = (bf16[2,16,384]{2,1,0:T(8,128)(2,1)S(1)}, bf16[2,16,384]{2,1,0:T(8,128)(2,1)S(1)}, u32[]{:S(2)}, u32[]{:S(2)}) collective-permute-start(bf16[2,16,384]{2,1,0:T(8,128)(2,1)S(1)} %slice_bitcast_fusion.41), channel_id=1, source_target_pairs={{0,16},{8,24},{16,0},{24,8},{1,17},{9,25},{17,1},{25,9},{2,18},{10... | collective-permute-start | bytes 73736 | tf_op jit(solution)/shard_map/ppermute | solution.py:1002
  (87 other events, 992.5 us)
Sparse Core Ops, SparseCore 0:
  11.5 67.5 all-gather.4
  82.6 80.0 all-gather.6
